TPU v7x, 32 devices: a whole 2x2x4 slice. The times are simulated.
32 devices in a mesh: rep: 4 (over y, x), fsdp: 2 (over core), tp: 4 (over z).
Axes of the slice: x: 2, y: 2, z: 4, core: 2. Of those that a mesh axis runs over, the one named last changes fastest.
Arguments:
- grad_parts: bfloat16 [2, 2, 8192, 1024], P('fsdp', None, 'rep', 'tp'), may hold values from -4 to 4
- master_weight: float32 [2, 8192, 1024], P(None, ('rep', 'fsdp'), 'tp'), may hold values from -0.0625 to 0.0625
- moment_one: float32 [2, 8192, 1024], P(None, ('rep', 'fsdp'), 'tp'), may hold values from -4 to 4
- moment_two: float32 [2, 8192, 1024], P(None, ('rep', 'fsdp'), 'tp'), may hold values from 0.1 to 2
- layer_inputs: bfloat16 [384, 4, 8192], P(('rep', 'fsdp'), None, 'tp'), may hold values from -6 to 6
- queries: bfloat16 [384, 4, 8192], P(('rep', 'fsdp'), None, 'tp'), may hold values from -105 to 105
- kv_cache: bfloat16 [384, 24, 2, 1024], P(('rep', 'fsdp'), None, None, 'tp'), may hold values from -4 to 4
- lengths: int32 [384], P(('rep', 'fsdp')), may hold values from 2 to 24
Outputs:
- new_master: float32 [2, 8192, 1024], P(None, ('rep', 'fsdp'), 'tp')
- new_moment_one: float32 [2, 8192, 1024], P(None, ('rep', 'fsdp'), 'tp')
- new_moment_two: float32 [2, 8192, 1024], P(None, ('rep', 'fsdp'), 'tp')
- context: bfloat16 [384, 4, 8192], P(('rep', 'fsdp'), None, 'tp')
Inputs may be any that keep to these rules, and one draw needn't show every extreme that they name: lengths[r] is the number of valid cached positions of row r, at most 24.
All inputs are finite; a program needn't handle non-finite values.
Results may differ from a plain program's by a relative error of at most 0.0065.
Values may be sent and summed in bfloat16 or wider, within the bound.
A program may use at most 64 MiB of HBM per device.

v0:
```python
import functools

import jax
import jax.numpy as jnp
from jax import lax
from jax.experimental import pallas as pl
from jax.experimental.pallas import tpu as pltpu
from jax.sharding import PartitionSpec as P

HD = 128
MESH = pl.DeviceIdType.MESH
W_CHUNKS = 4
ADAM_SUB = 32
TAIL_ROWS = 8
TAIL_BLOCKS = 3
LOG2E = 1.4426950408889634


def learner_kernel(
    sizes, grad_hbm, master_hbm, one_hbm, two_hbm, x_hbm, kv_hbm,
    fresh_out, cached_out, master_out, one_out, two_out,
    own_grad, peer_grad, master, one, two, wbuf, xbuf, xflat, acc, partner_acc, kv_raw, kv_flat,
    local_sem, out_sem, grad_send, grad_recv, x_send, x_recv, x_swap_send,
    w_send, w_recv, w_fwd_send, acc_send, acc_recv,
):
    n_tp, depth = sizes
    r, f, t = lax.axis_index("rep"), lax.axis_index("fsdp"), lax.axis_index("tp")
    nf = 1 - f
    rx = r + 1 - 2 * lax.rem(r, 2)
    ry = lax.rem(r + 2, 4)
    rd = lax.rem(rx + 2, 4)
    partner, dev_x, dev_y = (r, nf, t), (rx, f, t), (ry, f, t)
    up, down = (r, f, t + 1), (r, f, t - 1)
    chunk = depth // W_CHUNKS

    def half(index):
        return pl.ds(pl.multiple_of(index * depth, depth), depth)

    local = [
        pltpu.make_async_copy(grad_hbm.at[0, :, half(f), :], own_grad, local_sem.at[0]),
        pltpu.make_async_copy(master_hbm, master, local_sem.at[1]),
        pltpu.make_async_copy(one_hbm, one, local_sem.at[2]),
        pltpu.make_async_copy(two_hbm, two, local_sem.at[3]),
        pltpu.make_async_copy(x_hbm.at[:, :, half(f)], xbuf.at[t, f], local_sem.at[4]),
        pltpu.make_async_copy(kv_hbm, kv_raw, local_sem.at[5]),
    ]
    for copy in local:
        copy.start()

    barrier = pltpu.get_barrier_semaphore()
    for device in (partner, dev_x, dev_y):
        pl.semaphore_signal(barrier, inc=1, device_id=device, device_id_type=MESH)

    @pl.when(t < n_tp - 1)
    def _():
        pl.semaphore_signal(barrier, inc=1, device_id=up, device_id_type=MESH)

    @pl.when(t > 0)
    def _():
        pl.semaphore_signal(barrier, inc=1, device_id=down, device_id_type=MESH)

    pl.semaphore_wait(barrier, jnp.where((t > 0) & (t < n_tp - 1), 5, 4))

    def rows(c):
        return pl.ds(pl.multiple_of(c * chunk, chunk), chunk)

    def remote(src, dst, send, recv, device):
        return pltpu.make_async_remote_copy(
            src_ref=src, dst_ref=dst, send_sem=send, recv_sem=recv,
            device_id=device, device_id_type=MESH,
        )

    def grad_copy(c):
        source = pl.ds(pl.multiple_of(nf * depth + c * chunk, chunk), chunk)
        return remote(
            grad_hbm.at[0, :, source, :], peer_grad.at[:, rows(c), :],
            grad_send.at[c], grad_recv.at[c], partner,
        )

    def x_move(z, th, side):
        return remote(
            xbuf.at[z, th], xbuf.at[z, th], x_send.at[side, z, th], x_recv.at[z, th],
            up if side == 1 else down,
        )

    def x_own(side):
        return remote(
            x_hbm.at[:, :, half(f)], xbuf.at[t, f], x_send.at[side, t, f], x_recv.at[t, f],
            up if side == 1 else down,
        )

    x_swap = remote(x_hbm.at[:, :, half(nf)], xbuf.at[t, f], x_swap_send.at[0], x_recv.at[t, f], partner)

    def both_ways(act):
        @pl.when(t < n_tp - 1)
        def _():
            act(1)

        @pl.when(t > 0)
        def _():
            act(0)

    grad_copy(0).start()
    x_swap.start()
    both_ways(lambda side: x_own(side).start())
    for c in range(1, W_CHUNKS):
        grad_copy(c).start()

    def w_copy(c, way):
        return remote(
            wbuf.at[r, :, rows(c), :], wbuf.at[r, :, rows(c), :],
            w_send.at[way, c], w_recv.at[r, c], dev_x if way == 0 else dev_y,
        )

    def w_arrived(owner, c):
        remote(
            wbuf.at[owner, :, rows(c), :], wbuf.at[owner, :, rows(c), :],
            w_send.at[0, c], w_recv.at[owner, c], dev_x,
        ).wait_recv()

    def w_forward(c):
        owner, device = (rx, dev_y) if c % 2 == 0 else (ry, dev_x)
        return remote(
            wbuf.at[owner, :, rows(c), :], wbuf.at[owner, :, rows(c), :],
            w_fwd_send.at[c], w_recv.at[owner, c], device,
        )

    def x_arrived(z, th):
        x_move(z, th, 1).wait_recv()

    for copy in local[:4]:
        copy.wait()

    first_bias = 1.0 - 0.9**10
    second_bias = 1.0 - 0.95**10

    def adam(c):
        def sub(i, carry):
            at = pl.ds(pl.multiple_of(c * chunk + i * ADAM_SUB, ADAM_SUB), ADAM_SUB)
            gradient = own_grad[:, at, :].astype(jnp.float32) + peer_grad[:, at, :].astype(jnp.float32)
            new_one = 0.9 * one[:, at, :] + (1.0 - 0.9) * gradient
            new_two = 0.95 * two[:, at, :] + (1.0 - 0.95) * gradient * gradient
            update = new_one / first_bias / (jnp.sqrt(new_two / second_bias) + 1e-08)
            old = master[:, at, :]
            new_master = old - 0.001 * (update + 0.1 * old)
            one[:, at, :] = new_one
            two[:, at, :] = new_two
            master[:, at, :] = new_master
            wbuf[r, :, at, :] = new_master.astype(jnp.bfloat16)
            return carry

        lax.fori_loop(0, chunk // ADAM_SUB, sub, 0)

    for c in range(W_CHUNKS):
        grad_copy(c).wait_recv()
        adam(c)
        if c == 0:
            x_arrived(t, nf)
            both_ways(lambda side: x_move(t, nf, side).start())
        else:
            w_copy(c - 1, 0).start()
            w_copy(c - 1, 1).start()
    outs = [
        pltpu.make_async_copy(master, master_out, out_sem.at[0]),
        pltpu.make_async_copy(one, one_out, out_sem.at[1]),
        pltpu.make_async_copy(two, two_out, out_sem.at[2]),
    ]
    for copy in outs:
        copy.start()
    w_copy(W_CHUNKS - 1, 0).start()
    w_copy(W_CHUNKS - 1, 1).start()
    local[4].wait()
    local[5].wait()

    ends_up, ends_down = t + 1 == n_tp - 1, t == 1

    def x_wait(k, th):
        @pl.when(t - k >= 0)
        def _():
            x_arrived(t - k, th)

        @pl.when(t + k < n_tp)
        def _():
            x_arrived(t + k, th)

    def x_forward(k, th, go_up, go_down):
        @pl.when((t - k >= 0) & (t < n_tp - 1) & go_up)
        def _():
            x_move(t - k, th, 1).start()

        @pl.when((t + k < n_tp) & (t > 0) & go_down)
        def _():
            x_move(t + k, th, 0).start()

    def x_first_half():
        x_wait(1, f)
        x_forward(1, f, ends_up, ends_down)

    def x_second_half():
        x_wait(1, nf)
        x_forward(1, nf, True, True)
        x_forward(1, f, jnp.logical_not(ends_up), jnp.logical_not(ends_down))

    def x_far(k, th):
        x_wait(k, th)
        x_forward(k, th, True, True)

    def w_step(c):
        w_arrived(rx, c)
        w_arrived(ry, c)
        w_forward(c).start()

    kv_rows, cache_len = kv_raw.shape[:2]
    pieces = kv_rows // 8

    def split_cache(quarter):
        def body(i, carry):
            row = (quarter * pieces + i) * 2
            at = pl.ds(pl.multiple_of(row * cache_len, 2 * cache_len), 2 * cache_len)
            for j in range(2):
                kv_flat[j, at, :] = kv_raw[pl.ds(row, 2), :, j, :].reshape(2 * cache_len, -1)
            return carry

        lax.fori_loop(0, pieces, body, 0)

    split_cache(0)
    x_first_half()
    split_cache(1)
    w_step(0)
    split_cache(2)
    x_second_half()
    split_cache(3)
    cached_copy = pltpu.make_async_copy(kv_flat, cached_out, out_sem.at[3])
    cached_copy.start()
    w_step(1)
    w_step(2)
    x_far(2, nf)
    w_step(3)
    x_far(2, f)

    acc[...] = jnp.zeros_like(acc)

    x_rows = xbuf.shape[2]
    x_part = x_rows // 4
    flat_part = xflat.shape[0] // 4

    def multiply(z, th):
        def flatten(i, carry):
            at = pl.ds(pl.multiple_of(i * flat_part, flat_part), flat_part)
            xflat[at, :] = xbuf[z, th, pl.ds(i * x_part, x_part)].reshape(flat_part, depth)
            return carry

        lax.fori_loop(0, 4, flatten, 0, unroll=True)

        def one_side(kv, carry):
            acc[th, kv] += jnp.dot(xflat[...], wbuf[z, kv], preferred_element_type=jnp.float32)
            return carry

        lax.fori_loop(0, 2, one_side, 0, unroll=True)

    for c in range(W_CHUNKS):
        w_arrived(rd, c)

    def step(j, carry):
        k = j // 2
        th = nf + lax.rem(j, 2) * (1 - 2 * nf)

        def side(s, inner):
            z = t + (2 * s - 1) * k

            @pl.when((z >= 0) & (z < n_tp))
            def _():
                @pl.when(k == n_tp - 1)
                def _():
                    x_arrived(z, th)

                multiply(z, th)

            return inner

        lax.fori_loop(jnp.where(k == 0, 1, 0), 2, side, 0)
        return carry

    lax.fori_loop(0, 2 * n_tp - 1, step, 0)

    swap = remote(acc.at[nf], partner_acc, acc_send.at[0], acc_recv.at[0], partner)
    swap.start()
    step(2 * n_tp - 1, 0)
    for c in range(W_CHUNKS):
        grad_copy(c).wait_send()
        w_copy(c, 0).wait_send()
        w_copy(c, 1).wait_send()
        w_forward(c).wait_send()
    x_swap.wait_send()
    both_ways(lambda side: x_own(side).wait_send())
    both_ways(lambda side: x_move(t, nf, side).wait_send())
    for k in range(1, n_tp - 1):
        for th in (f, nf):
            @pl.when((t - k >= 0) & (t < n_tp - 1))
            def _():
                x_move(t - k, th, 1).wait_send()

            @pl.when((t + k < n_tp) & (t > 0))
            def _():
                x_move(t + k, th, 0).wait_send()
    for copy in outs:
        copy.wait()
    cached_copy.wait()
    swap.wait_recv()
    fresh_out[...] = (acc[f] + partner_acc[...]).astype(jnp.bfloat16)
    swap.wait_send()


def tail_kernel(
    lengths, q_ref, kv_ref, fresh_in, master_in, one_in, two_in,
    context, master_out, one_out, two_out, fresh_ref, sem,
):
    block = pl.program_id(0)
    moves = [
        pltpu.make_async_copy(master_in, master_out, sem.at[1]),
        pltpu.make_async_copy(one_in, one_out, sem.at[2]),
        pltpu.make_async_copy(two_in, two_out, sem.at[3]),
    ]

    @pl.when(block == 0)
    def _():
        fresh_copy = pltpu.make_async_copy(fresh_in, fresh_ref, sem.at[0])
        fresh_copy.start()
        for move in moves:
            move.start()
        fresh_copy.wait()

    step_rows, step_count, features = q_ref.shape
    row_count = TAIL_ROWS
    head = HD
    cache_len = kv_ref.shape[1] // step_rows
    cached = row_count * cache_len
    tokens = row_count * step_count
    keys = cached + tokens
    groups = fresh_ref.shape[2] // head
    per_group = features // head // groups
    column = lax.broadcasted_iota(jnp.int32, (1, keys), 1)
    is_old = column < cached
    new_column = column - cached
    key_row = jnp.where(is_old, column // cache_len, new_column // step_count)
    position = column - key_row * cache_len
    new_row = jnp.where(is_old, -1, key_row)
    token = lax.broadcasted_iota(jnp.int32, (tokens, 1), 0)
    row = token // step_count
    new_valid = (new_row == row) & (new_column <= token)
    low = -0.7 * float(jnp.finfo(jnp.float32).max)
    factor = head**-0.5 * LOG2E
    contract = (((1,), (1,)), ((), ()))
    for part in range(step_rows // row_count):
        first_row = part * row_count
        start = block * step_rows + first_row
        limit = jnp.zeros((1, keys), jnp.int32)
        for at in range(row_count):
            limit = jnp.where(key_row == at, lengths[start + at], limit)
        valid = (jnp.where(is_old & (position < limit), key_row, -1) == row) | new_valid
        here = pl.ds(pl.multiple_of(start * step_count, tokens), tokens)
        old = slice(first_row * cache_len, first_row * cache_len + cached)
        mine = slice(first_row, first_row + row_count)
        for group in range(groups):
            cols = slice(group * head, (group + 1) * head)
            query = jnp.concatenate(
                [
                    q_ref[mine, :, (group * per_group + h) * head : (group * per_group + h + 1) * head].reshape(
                        tokens, head
                    )
                    for h in range(per_group)
                ],
                axis=0,
            )
            key = jnp.concatenate([kv_ref[0, old, cols], fresh_ref[0, here, cols]], axis=0)
            value = jnp.concatenate([kv_ref[1, old, cols], fresh_ref[1, here, cols]], axis=0)
            scores = lax.dot_general(query, key, contract, preferred_element_type=jnp.float32)
            scores = jnp.where(valid[None], scores.reshape(per_group, tokens, keys), low)
            weights = jnp.exp2((scores - jnp.max(scores, axis=-1, keepdims=True)) * factor)
            weights = weights * (1.0 / jnp.sum(weights, axis=-1, keepdims=True))
            weights = weights.astype(jnp.bfloat16).reshape(per_group * tokens, keys)
            out = jnp.dot(weights, value, preferred_element_type=jnp.float32)
            for h in range(per_group):
                at = (group * per_group + h) * head
                piece = out[h * tokens : (h + 1) * tokens].reshape(row_count, step_count, head)
                context[mine, :, at : at + head] = piece.astype(jnp.bfloat16)

    @pl.when(block == pl.num_programs(0) - 1)
    def _():
        for move in moves:
            move.wait()


def fused_device(n_rep, grad_parts, master_weight, moment_one, moment_two, layer_inputs, queries, kv_cache, lengths):
    row_count, step_count, features = layer_inputs.shape
    _, depth, width = master_weight.shape
    n_tp = n_rep
    tokens = row_count * step_count
    cache_len = kv_cache.shape[1]
    bf16, f32 = jnp.bfloat16, jnp.float32
    dma = pltpu.SemaphoreType.DMA
    state = jax.ShapeDtypeStruct(master_weight.shape, f32)
    any_spec = pl.BlockSpec(memory_space=pl.ANY)
    hbm_spec = pl.BlockSpec(memory_space=pltpu.HBM)
    in_place = [
        pltpu.with_memory_space_constraint(array, pltpu.HBM)
        for array in (grad_parts, master_weight, moment_one, moment_two, layer_inputs, kv_cache)
    ]
    fresh, cached, master, one, two = pl.pallas_call(
        functools.partial(learner_kernel, (n_tp, depth)),
        out_shape=(
            jax.ShapeDtypeStruct((2, tokens, width), bf16),
            jax.ShapeDtypeStruct((2, row_count * cache_len, width), bf16),
            state,
            state,
            state,
        ),
        in_specs=[hbm_spec] * 6,
        out_specs=(pl.BlockSpec(memory_space=pltpu.VMEM), hbm_spec, any_spec, any_spec, any_spec),
        scratch_shapes=[
            pltpu.VMEM((2, depth, width), bf16),
            pltpu.VMEM((2, depth, width), bf16),
            pltpu.VMEM((2, depth, width), f32),
            pltpu.VMEM((2, depth, width), f32),
            pltpu.VMEM((2, depth, width), f32),
            pltpu.VMEM((n_rep, 2, depth, width), bf16),
            pltpu.VMEM((n_tp, 2, row_count, step_count, depth), bf16),
            pltpu.VMEM((tokens, depth), bf16),
            pltpu.VMEM((2, 2, tokens, width), f32),
            pltpu.VMEM((2, tokens, width), f32),
            pltpu.VMEM(kv_cache.shape, bf16),
            pltpu.VMEM((2, row_count * cache_len, width), bf16),
            dma((6,)),
            dma((4,)),
            dma((W_CHUNKS,)),
            dma((W_CHUNKS,)),
            dma((2, n_tp, 2)),
            dma((n_tp, 2)),
            dma((1,)),
            dma((2, W_CHUNKS)),
            dma((n_rep, W_CHUNKS)),
            dma((W_CHUNKS,)),
            dma((1,)),
            dma((1,)),
        ],
        compiler_params=pltpu.CompilerParams(
            collective_id=0, has_side_effects=True, vmem_limit_bytes=36 * 1024 * 1024
        ),
    )(*in_place)
    step_rows = TAIL_ROWS * TAIL_BLOCKS
    token_spec = pl.BlockSpec((step_rows, step_count, features), lambda i, *_: (i, 0, 0))
    context, master, one, two = pl.pallas_call(
        tail_kernel,
        out_shape=(jax.ShapeDtypeStruct(queries.shape, bf16), state, state, state),
        grid_spec=pltpu.PrefetchScalarGridSpec(
            num_scalar_prefetch=1,
            grid=(row_count // step_rows,),
            in_specs=[
                token_spec,
                pl.BlockSpec((2, step_rows * cache_len, width), lambda i, *_: (0, i, 0)),
                any_spec,
                any_spec,
                any_spec,
                any_spec,
            ],
            out_specs=(token_spec, hbm_spec, hbm_spec, hbm_spec),
            scratch_shapes=[pltpu.VMEM((2, tokens, width), bf16), dma((4,))],
        ),
        compiler_params=pltpu.CompilerParams(
            dimension_semantics=("arbitrary",), vmem_limit_bytes=16 * 1024 * 1024
        ),
    )(lengths, queries, cached, fresh, master, one, two)
    return (master, one, two, context)


beta_one = 0.9
beta_two = 0.95
learning_rate = 0.001
weight_decay = 0.1
epsilon = 1e-08
first_bias = 1.0 - 0.9**10
second_bias = 1.0 - 0.95**10


def adamw_update(gradient, master, moment_one, moment_two):
    new_one = beta_one * moment_one + (1.0 - beta_one) * gradient
    new_two = beta_two * moment_two + (1.0 - beta_two) * gradient * gradient
    update = new_one / first_bias / (jnp.sqrt(new_two / second_bias) + epsilon)
    new_master = master - learning_rate * (update + weight_decay * master)
    return (new_one, new_two, new_master)


def attend(queries, kv_cache, fresh_keys, fresh_values, lengths):
    row_count = queries.shape[0]
    step_count = queries.shape[1]
    kv_heads = fresh_keys.shape[2]
    cache_len = kv_cache.shape[1]
    grouped = queries.reshape(row_count, step_count, kv_heads, -1, HD)
    cached_keys = kv_cache[:, :, 0].reshape(row_count, cache_len, kv_heads, HD)
    cached_values = kv_cache[:, :, 1].reshape(row_count, cache_len, kv_heads, HD)
    scaling = 1.0 / jnp.sqrt(jnp.float32(HD))
    cached_scores = (
        jnp.einsum("rsgqd,rcgd->rsgqc", grouped, cached_keys, preferred_element_type=jnp.float32)
        * scaling
    )
    fresh_scores = (
        jnp.einsum("rsgqd,rugd->rsgqu", grouped, fresh_keys, preferred_element_type=jnp.float32)
        * scaling
    )
    valid_old = jnp.arange(cache_len, dtype=jnp.int32)[None, :] < lengths[:, None]
    valid_old = valid_old[:, None, None, None, :]
    steps_index = jnp.arange(step_count, dtype=jnp.int32)
    valid_new = (steps_index[None, :] <= steps_index[:, None])[None, :, None, None, :]
    scores = jnp.concatenate(
        [
            jnp.where(valid_old, cached_scores, -jnp.inf),
            jnp.where(valid_new, fresh_scores, -jnp.inf),
        ],
        axis=-1,
    )
    row_max = jnp.max(scores, axis=-1, keepdims=True)
    exponent = jnp.exp(scores - row_max)
    weights = (exponent / jnp.sum(exponent, axis=-1, keepdims=True)).astype(jnp.bfloat16)
    output = jnp.einsum(
        "rsgqc,rcgd->rsgqd",
        weights[..., :cache_len],
        cached_values,
        preferred_element_type=jnp.float32,
    )
    output = output + jnp.einsum(
        "rsgqu,rugd->rsgqd",
        weights[..., cache_len:],
        fresh_values,
        preferred_element_type=jnp.float32,
    )
    return output.astype(jnp.bfloat16).reshape(row_count, step_count, -1)


def on_device(
    grad_parts, master_weight, moment_one, moment_two, layer_inputs, queries, kv_cache, lengths
):
    gradient = lax.psum_scatter(
        grad_parts[0].astype(jnp.float32).astype(jnp.bfloat16),
        "fsdp",
        scatter_dimension=1,
        tiled=True,
    ).astype(jnp.float32)
    new_one, new_two, new_master = adamw_update(gradient, master_weight, moment_one, moment_two)
    rollout_weight = new_master.astype(jnp.bfloat16)
    row_count = layer_inputs.shape[0]
    step_count = layer_inputs.shape[1]
    gathered = lax.all_gather(layer_inputs, "tp", axis=2, tiled=True)
    flattened = gathered.reshape(row_count * step_count, gathered.shape[2])
    projected = jnp.einsum(
        "td,kdc->ktc",
        flattened,
        lax.all_gather(rollout_weight, ("rep", "fsdp"), axis=1, tiled=True),
        preferred_element_type=jnp.float32,
    )
    fresh_pair = projected.astype(jnp.bfloat16).reshape(2, row_count, step_count, -1, HD)
    context = attend(queries, kv_cache, fresh_pair[0], fresh_pair[1], lengths)
    return (new_master, new_one, new_two, context)


def solution(mesh):
    shape = mesh.shape
    fits = shape["rep"] == 4 and shape["tp"] == 4 and shape["fsdp"] == 2
    run = functools.partial(fused_device, shape["rep"]) if fits else on_device
    return jax.shard_map(
        run,
        mesh=mesh,
        in_specs=(
            P("fsdp", None, "rep", "tp"),
            P(None, ("rep", "fsdp"), "tp"),
            P(None, ("rep", "fsdp"), "tp"),
            P(None, ("rep", "fsdp"), "tp"),
            P(("rep", "fsdp"), None, "tp"),
            P(("rep", "fsdp"), None, "tp"),
            P(("rep", "fsdp"), None, None, "tp"),
            P(("rep", "fsdp")),
        ),
        out_specs=(
            P(None, ("rep", "fsdp"), "tp"),
            P(None, ("rep", "fsdp"), "tp"),
            P(None, ("rep", "fsdp"), "tp"),
            P(("rep", "fsdp"), None, "tp"),
        ),
        check_vma=False,
    )
```

profile of v0, /device:TPU:0, one launch (start us, length us, event | category | flops | bytes accessed | tf_op | source)
XLA Modules:
  0.0 62.1 jit_solution(6584884779032806878)
XLA Ops:
  0.6 0.0 copy-start.1
  0.6 0.0 copy-start
  0.7 57.0 %shard_map.111 = (bf16[2,192,256]{2,1,0:T(8,128)(2,1)S(1)}, bf16[2,1152,256]{2,1,0:T(8,128)(2,1)S(1)}, f32[2,1024,256]{2,1,0:T(8,128)S(1)}, f32[2,1024,256]{2,1,0:T(8,128)S(1)}, f32[2,1024,256]{2,1,0:T(8,128)S(1)}) custom-call(bf16[1,2,2048,256]{3,2,1,0:T(8,128)(2,1)} %grad_hbm.1, f32[2,1024,256]{2,1,0:T(8,128)} %master_hbm.1, f32[2,1024,256]{2,1,0:T(8,128)} %one_hbm.1, ...), custom_call_target="tpu_custom_call" | custom-call | tf_op jit(solution)/shard_map/pallas_call | solution.py:409
  57.7 0.0 copy-done.1
  57.7 0.0 copy-done
  57.7 4.4 %shard_map.112 = (bf16[48,4,2048]{2,1,0:T(4,128)(2,1)}, f32[2,1024,256]{2,1,0:T(8,128)}, f32[2,1024,256]{2,1,0:T(8,128)}, f32[2,1024,256]{2,1,0:T(8,128)}) custom-call(s32[48]{0:T(128)S(1)} %copy-done.1, bf16[48,4,2048]{2,1,0:T(4,128)(2,1)S(1)} %copy-done, bf16[2,1152,256]{2,1,0:T(8,128)(2,1)S(1)} %get-tuple-element.13.kv_ref, ...), custom_call_target="tpu_custom_call" | custom-call | tf_op jit(solution)/shard_map/pallas_call | solution.py:452
Async XLA Ops:
  0.6 57.1 %copy-start.1 = (s32[48]{0:T(128)S(1)}, s32[48]{0:T(128)}, u32[]{:S(2)}) copy-start(s32[48]{0:T(128)} %lengths.1) | copy-start | bytes 580
  0.6 57.1 %copy-start = (bf16[48,4,2048]{2,1,0:T(4,128)(2,1)S(1)}, bf16[48,4,2048]{2,1,0:T(4,128)(2,1)}, u32[]{:S(2)}) copy-start(bf16[48,4,2048]{2,1,0:T(4,128)(2,1)} %q_ref.1) | copy-start | bytes 2359300
where the time goes:
time: 62.3 us; the launch traced here: 62.1 us
  Pallas kernels  61.5 us (99%)
  between operations  0.67 us (1%)
    pallas_call x1, Pallas kernels, fused_device(): pl.pallas_call(functools.partial(learner_kernel, (n_tp, depth)), out_shap...  57 us
    pallas_call x1, Pallas kernels, fused_device(): pl.pallas_call(tail_kernel, out_shape=(jax.ShapeDtypeStruct(queries.shape...  4.42 us

commit v1 on v0

--- a/solution.py
+++ b/solution.py
@@ -9,7 +9,8 @@
 
 HD = 128
 MESH = pl.DeviceIdType.MESH
-W_CHUNKS = 4
+W_CHUNKS = 2
+GROUPS = 4
 ADAM_SUB = 32
 TAIL_ROWS = 8
 TAIL_BLOCKS = 3
@@ -17,52 +18,79 @@
 
 
 def learner_kernel(
-    sizes, grad_hbm, master_hbm, one_hbm, two_hbm, x_hbm, kv_hbm,
+    grad_hbm, master_hbm, one_hbm, two_hbm, x_hbm, kv_hbm,
     fresh_out, cached_out, master_out, one_out, two_out,
-    own_grad, peer_grad, master, one, two, wbuf, xbuf, xflat, acc, partner_acc, kv_raw, kv_flat,
-    local_sem, out_sem, grad_send, grad_recv, x_send, x_recv, x_swap_send,
-    w_send, w_recv, w_fwd_send, acc_send, acc_recv,
+    own_grad, peer_grad, master, one, two, wpair, wbuf, xbuf, xflat,
+    far, far_peer, far_out, far_in, near, near_peer, kv_raw, kv_flat,
+    grad_sem, state_sem, x_sem, kv_sem, out_sem, grad_send, grad_recv, x_send, x_recv,
+    pair_send, pair_recv, w_send, w_recv, w_fwd_send, far_send, far_recv, back_send, back_recv, near_send, near_recv,
 ):
-    n_tp, depth = sizes
     r, f, t = lax.axis_index("rep"), lax.axis_index("fsdp"), lax.axis_index("tp")
     nf = 1 - f
     rx = r + 1 - 2 * lax.rem(r, 2)
     ry = lax.rem(r + 2, 4)
     rd = lax.rem(rx + 2, 4)
     partner, dev_x, dev_y = (r, nf, t), (rx, f, t), (ry, f, t)
-    up, down = (r, f, t + 1), (r, f, t - 1)
-    chunk = depth // W_CHUNKS
-
-    def half(index):
-        return pl.ds(pl.multiple_of(index * depth, depth), depth)
-
-    local = [
-        pltpu.make_async_copy(grad_hbm.at[0, :, half(f), :], own_grad, local_sem.at[0]),
-        pltpu.make_async_copy(master_hbm, master, local_sem.at[1]),
-        pltpu.make_async_copy(one_hbm, one, local_sem.at[2]),
-        pltpu.make_async_copy(two_hbm, two, local_sem.at[3]),
-        pltpu.make_async_copy(x_hbm.at[:, :, half(f)], xbuf.at[t, f], local_sem.at[4]),
-        pltpu.make_async_copy(kv_hbm, kv_raw, local_sem.at[5]),
-    ]
-    for copy in local:
-        copy.start()
+    pair = t + 1 - 2 * lax.rem(t, 2)
+    mirror = 3 - t
+    pair_mirror = 3 - pair
+    middle = (t == 1) | (t == 2)
+    mine = lax.rem((t + 1) // 2, 2)
+    theirs = 1 - mine
+    depth = master.shape[1]
+    half = depth // 2
+    chunk = half // W_CHUNKS
+    x_rows, x_steps = xbuf.shape[2:4]
+    group_rows = x_rows // GROUPS
+    group_tokens = group_rows * x_steps
+    blocks = wbuf.shape[2] // half
+
+    def state_rows(sub, c):
+        return pl.ds(pl.multiple_of(sub * half + c * chunk, chunk), chunk)
+
+    def owner_rows(owner, c):
+        return pl.ds(pl.multiple_of(owner * half + c * chunk, chunk), chunk)
+
+    order = []
+    for c in range(W_CHUNKS):
+        order += [(theirs, c), (mine, c)]
+
+    def features(h, sub):
+        return pl.ds(pl.multiple_of(h * depth + sub * half, half), half)
+
+    def some_rows(g):
+        return pl.ds(g * group_rows, group_rows)
+
+    def tokens(g):
+        return pl.ds(pl.multiple_of(g * group_tokens, group_tokens), group_tokens)
+
+    grad_local, state_local = [], []
+    for i, (sub, c) in enumerate(order):
+        at = state_rows(sub, c)
+        source = pl.ds(pl.multiple_of(f * depth + sub * half + c * chunk, chunk), chunk)
+        grad_local.append(
+            pltpu.make_async_copy(grad_hbm.at[0, :, source, :], own_grad.at[:, at, :], grad_sem.at[i])
+        )
+        state_local.append([
+            pltpu.make_async_copy(hbm.at[:, at, :], vmem.at[:, at, :], state_sem.at[j, i])
+            for j, (hbm, vmem) in enumerate(((master_hbm, master), (one_hbm, one), (two_hbm, two)))
+        ])
+        grad_local[i].start()
+        for copy in state_local[i]:
+            copy.start()
+    x_local = pltpu.make_async_copy(x_hbm.at[:, :, features(f, mine)], xbuf.at[t, f], x_sem.at[0])
+    kv_local = pltpu.make_async_copy(kv_hbm, kv_raw, kv_sem.at[0])
+    x_local.start()
+    kv_local.start()
 
     barrier = pltpu.get_barrier_semaphore()
-    for device in (partner, dev_x, dev_y):
+    friends = [partner, dev_x, dev_y]
+    for i in range(1, blocks):
+        for h in range(2):
+            friends.append((r, h, lax.rem(t + i, blocks)))
+    for device in friends:
         pl.semaphore_signal(barrier, inc=1, device_id=device, device_id_type=MESH)
-
-    @pl.when(t < n_tp - 1)
-    def _():
-        pl.semaphore_signal(barrier, inc=1, device_id=up, device_id_type=MESH)
-
-    @pl.when(t > 0)
-    def _():
-        pl.semaphore_signal(barrier, inc=1, device_id=down, device_id_type=MESH)
-
-    pl.semaphore_wait(barrier, jnp.where((t > 0) & (t < n_tp - 1), 5, 4))
-
-    def rows(c):
-        return pl.ds(pl.multiple_of(c * chunk, chunk), chunk)
+    pl.semaphore_wait(barrier, len(friends))
 
     def remote(src, dst, send, recv, device):
         return pltpu.make_async_remote_copy(
@@ -70,73 +98,115 @@
             device_id=device, device_id_type=MESH,
         )
 
-    def grad_copy(c):
-        source = pl.ds(pl.multiple_of(nf * depth + c * chunk, chunk), chunk)
-        return remote(
-            grad_hbm.at[0, :, source, :], peer_grad.at[:, rows(c), :],
-            grad_send.at[c], grad_recv.at[c], partner,
-        )
-
-    def x_move(z, th, side):
-        return remote(
-            xbuf.at[z, th], xbuf.at[z, th], x_send.at[side, z, th], x_recv.at[z, th],
-            up if side == 1 else down,
-        )
-
-    def x_own(side):
-        return remote(
-            x_hbm.at[:, :, half(f)], xbuf.at[t, f], x_send.at[side, t, f], x_recv.at[t, f],
-            up if side == 1 else down,
-        )
-
-    x_swap = remote(x_hbm.at[:, :, half(nf)], xbuf.at[t, f], x_swap_send.at[0], x_recv.at[t, f], partner)
-
-    def both_ways(act):
-        @pl.when(t < n_tp - 1)
+    def grad_copy(i):
+        sub, c = order[i]
+        source = pl.ds(pl.multiple_of(nf * depth + sub * half + c * chunk, chunk), chunk)
+        return remote(
+            grad_hbm.at[0, :, source, :], peer_grad.at[:, state_rows(sub, c), :],
+            grad_send.at[i], grad_recv.at[i], partner,
+        )
+
+    def x_own(g, h, sub, slot, device):
+        return remote(
+            x_hbm.at[some_rows(g), :, features(h, sub)], xbuf.at[t, f, some_rows(g)],
+            x_send.at[slot, g], x_recv.at[t, f, g], device,
+        )
+
+    def x_swap(g):
+        return x_own(g, nf, mine, 0, partner)
+
+    def x_mirror(g, h):
+        return x_own(g, h, mine, 1 + h, (r, h, mirror))
+
+    def x_pair(g, h):
+        return x_own(g, h, theirs, 3 + h, (r, h, pair))
+
+    def x_pair_mirror(g, h):
+        return x_own(g, h, theirs, 5 + h, (r, h, pair_mirror))
+
+    def x_relay(g, th):
+        return remote(
+            xbuf.at[pair, th, some_rows(g)], xbuf.at[pair, th, some_rows(g)],
+            x_send.at[7 + th, g], x_recv.at[pair, th, g], (r, f, mirror),
+        )
+
+    def x_arrived(k, th, g):
+        remote(
+            xbuf.at[k, th, some_rows(g)], xbuf.at[k, th, some_rows(g)],
+            x_send.at[0, g], x_recv.at[k, th, g], partner,
+        ).wait_recv()
+
+    def x_out(g):
+        for h in range(2):
+            x_pair(g, h).start()
+        for h in range(2):
+            x_mirror(g, h).start()
+
+        @pl.when(middle)
         def _():
-            act(1)
-
-        @pl.when(t > 0)
+            for h in range(2):
+                x_pair_mirror(g, h).start()
+
+    def relay(g):
+        for th in range(2):
+            x_arrived(pair, th, g)
+
+        @pl.when(middle)
         def _():
-            act(0)
+            for th in range(2):
+                x_relay(g, th).start()
+
+    def w_pair(c):
+        return remote(
+            wpair.at[:, pl.ds(c * chunk, chunk), :], wbuf.at[1, :, owner_rows(r, c), :],
+            pair_send.at[c], pair_recv.at[c], (r, f, pair),
+        )
+
+    def w_copy(cg, c, way):
+        return remote(
+            wbuf.at[cg, :, owner_rows(r, c), :], wbuf.at[cg, :, owner_rows(r, c), :],
+            w_send.at[cg, way, c], w_recv.at[cg, r, c], dev_x if way == 0 else dev_y,
+        )
+
+    def w_arrived(cg, owner, c):
+        remote(
+            wbuf.at[cg, :, owner_rows(owner, c), :], wbuf.at[cg, :, owner_rows(owner, c), :],
+            w_send.at[cg, 0, c], w_recv.at[cg, owner, c], dev_x,
+        ).wait_recv()
+
+    def w_forward(cg, c):
+        owner, device = (rx, dev_y) if c % 2 == 0 else (ry, dev_x)
+        return remote(
+            wbuf.at[cg, :, owner_rows(owner, c), :], wbuf.at[cg, :, owner_rows(owner, c), :],
+            w_fwd_send.at[cg, c], w_recv.at[cg, owner, c], device,
+        )
+
+    def w_go(cg, c):
+        w_copy(cg, c, 0).start()
+        w_copy(cg, c, 1).start()
+
+    def w_step(cg, c):
+        w_arrived(cg, rx, c)
+        w_arrived(cg, ry, c)
+        w_forward(cg, c).start()
+
+    def pair_step(c):
+        w_pair(c).wait_recv()
+        w_go(1, c)
 
     grad_copy(0).start()
-    x_swap.start()
-    both_ways(lambda side: x_own(side).start())
-    for c in range(1, W_CHUNKS):
-        grad_copy(c).start()
-
-    def w_copy(c, way):
-        return remote(
-            wbuf.at[r, :, rows(c), :], wbuf.at[r, :, rows(c), :],
-            w_send.at[way, c], w_recv.at[r, c], dev_x if way == 0 else dev_y,
-        )
-
-    def w_arrived(owner, c):
-        remote(
-            wbuf.at[owner, :, rows(c), :], wbuf.at[owner, :, rows(c), :],
-            w_send.at[0, c], w_recv.at[owner, c], dev_x,
-        ).wait_recv()
-
-    def w_forward(c):
-        owner, device = (rx, dev_y) if c % 2 == 0 else (ry, dev_x)
-        return remote(
-            wbuf.at[owner, :, rows(c), :], wbuf.at[owner, :, rows(c), :],
-            w_fwd_send.at[c], w_recv.at[owner, c], device,
-        )
-
-    def x_arrived(z, th):
-        x_move(z, th, 1).wait_recv()
-
-    for copy in local[:4]:
-        copy.wait()
+    x_out(0)
+    for i in range(1, len(order)):
+        grad_copy(i).start()
+    for g in range(GROUPS):
+        x_swap(g).start()
 
     first_bias = 1.0 - 0.9**10
     second_bias = 1.0 - 0.95**10
 
-    def adam(c):
-        def sub(i, carry):
-            at = pl.ds(pl.multiple_of(c * chunk + i * ADAM_SUB, ADAM_SUB), ADAM_SUB)
+    def adam(sub, c, out, base):
+        def piece(i, carry):
+            at = pl.ds(pl.multiple_of(sub * half + c * chunk + i * ADAM_SUB, ADAM_SUB), ADAM_SUB)
             gradient = own_grad[:, at, :].astype(jnp.float32) + peer_grad[:, at, :].astype(jnp.float32)
             new_one = 0.9 * one[:, at, :] + (1.0 - 0.9) * gradient
             new_two = 0.95 * two[:, at, :] + (1.0 - 0.95) * gradient * gradient
@@ -146,20 +216,26 @@
             one[:, at, :] = new_one
             two[:, at, :] = new_two
             master[:, at, :] = new_master
-            wbuf[r, :, at, :] = new_master.astype(jnp.bfloat16)
+            to = pl.ds(pl.multiple_of(base + c * chunk + i * ADAM_SUB, ADAM_SUB), ADAM_SUB)
+            out[:, to, :] = new_master.astype(jnp.bfloat16)
             return carry
 
-        lax.fori_loop(0, chunk // ADAM_SUB, sub, 0)
-
-    for c in range(W_CHUNKS):
-        grad_copy(c).wait_recv()
-        adam(c)
-        if c == 0:
-            x_arrived(t, nf)
-            both_ways(lambda side: x_move(t, nf, side).start())
+        lax.fori_loop(0, chunk // ADAM_SUB, piece, 0)
+
+    for i, (sub, c) in enumerate(order):
+        grad_local[i].wait()
+        for copy in state_local[i]:
+            copy.wait()
+        grad_copy(i).wait_recv()
+        if i % 2 == 0:
+            adam(sub, c, wpair, 0)
+            w_pair(c).start()
         else:
-            w_copy(c - 1, 0).start()
-            w_copy(c - 1, 1).start()
+            adam(sub, c, wbuf.at[0], r * half)
+            if c < W_CHUNKS // 2:
+                w_go(0, c)
+    for g in range(1, GROUPS):
+        x_out(g)
     outs = [
         pltpu.make_async_copy(master, master_out, out_sem.at[0]),
         pltpu.make_async_copy(one, one_out, out_sem.at[1]),
@@ -167,48 +243,8 @@
     ]
     for copy in outs:
         copy.start()
-    w_copy(W_CHUNKS - 1, 0).start()
-    w_copy(W_CHUNKS - 1, 1).start()
-    local[4].wait()
-    local[5].wait()
-
-    ends_up, ends_down = t + 1 == n_tp - 1, t == 1
-
-    def x_wait(k, th):
-        @pl.when(t - k >= 0)
-        def _():
-            x_arrived(t - k, th)
-
-        @pl.when(t + k < n_tp)
-        def _():
-            x_arrived(t + k, th)
-
-    def x_forward(k, th, go_up, go_down):
-        @pl.when((t - k >= 0) & (t < n_tp - 1) & go_up)
-        def _():
-            x_move(t - k, th, 1).start()
-
-        @pl.when((t + k < n_tp) & (t > 0) & go_down)
-        def _():
-            x_move(t + k, th, 0).start()
-
-    def x_first_half():
-        x_wait(1, f)
-        x_forward(1, f, ends_up, ends_down)
-
-    def x_second_half():
-        x_wait(1, nf)
-        x_forward(1, nf, True, True)
-        x_forward(1, f, jnp.logical_not(ends_up), jnp.logical_not(ends_down))
-
-    def x_far(k, th):
-        x_wait(k, th)
-        x_forward(k, th, True, True)
-
-    def w_step(c):
-        w_arrived(rx, c)
-        w_arrived(ry, c)
-        w_forward(c).start()
+    x_local.wait()
+    kv_local.wait()
 
     kv_rows, cache_len = kv_raw.shape[:2]
     pieces = kv_rows // 8
@@ -223,92 +259,139 @@
 
         lax.fori_loop(0, pieces, body, 0)
 
+    relay(0)
     split_cache(0)
-    x_first_half()
     split_cache(1)
-    w_step(0)
+    for c in range(W_CHUNKS // 2):
+        w_step(0, c)
+    for c in range(W_CHUNKS):
+        pair_step(c)
+    for c in range(W_CHUNKS // 2, W_CHUNKS):
+        w_go(0, c)
+    relay(1)
     split_cache(2)
-    x_second_half()
     split_cache(3)
     cached_copy = pltpu.make_async_copy(kv_flat, cached_out, out_sem.at[3])
     cached_copy.start()
-    w_step(1)
-    w_step(2)
-    x_far(2, nf)
-    w_step(3)
-    x_far(2, f)
-
-    acc[...] = jnp.zeros_like(acc)
-
-    x_rows = xbuf.shape[2]
-    x_part = x_rows // 4
-    flat_part = xflat.shape[0] // 4
-
-    def multiply(z, th):
-        def flatten(i, carry):
-            at = pl.ds(pl.multiple_of(i * flat_part, flat_part), flat_part)
-            xflat[at, :] = xbuf[z, th, pl.ds(i * x_part, x_part)].reshape(flat_part, depth)
+    for c in range(W_CHUNKS // 2):
+        w_step(1, c)
+    relay(2)
+    for c in range(W_CHUNKS // 2, W_CHUNKS):
+        w_step(1, c)
+    relay(3)
+    for c in range(W_CHUNKS):
+        w_arrived(1, rd, c)
+
+    def far_swap(g):
+        return remote(
+            far.at[nf, :, tokens(g), :], far_peer.at[:, tokens(g), :], far_send.at[g], far_recv.at[g], partner
+        )
+
+    def far_back(g):
+        return remote(
+            far_out.at[:, tokens(g), :], far_in.at[:, tokens(g), :], back_send.at[g], back_recv.at[g], (r, f, pair)
+        )
+
+    def far_step(g, carry):
+        x_arrived(t, nf, g)
+        for th in range(2):
+            x_arrived(mirror, th, g)
+            x_arrived(pair_mirror, th, g)
+
+        def flatten(k, inner):
+            for th in range(2):
+                piece = xbuf[k, th, pl.ds(g * group_rows, group_rows)].reshape(group_tokens, half)
+                xflat[th, tokens(g), pl.ds(pl.multiple_of(k * half, half), half)] = piece
+            return inner
+
+        lax.fori_loop(0, blocks, flatten, 0)
+        lhs = jnp.concatenate([xflat[0, tokens(g), :], xflat[1, tokens(g), :]], axis=0)
+        for kv in range(2):
+            product = jnp.dot(lhs, wbuf[1, kv], preferred_element_type=jnp.float32)
+            for th in range(2):
+                far[th, kv, tokens(g), :] = product[th * group_tokens : (th + 1) * group_tokens]
+        far_swap(g).start()
+        return carry
+
+    def far_done(g):
+        far_swap(g).wait_recv()
+        far_out[:, tokens(g), :] = far[f, :, tokens(g), :] + far_peer[:, tokens(g), :]
+        far_back(g).start()
+
+    def far_loop(g, carry):
+        far_step(g, 0)
+
+        @pl.when(g > 0)
+        def _():
+            far_done(g - 1)
+
+        @pl.when(g == 1)
+        def _():
+            for c in range(W_CHUNKS // 2, W_CHUNKS):
+                w_step(0, c)
+
+        return carry
+
+    lax.fori_loop(0, GROUPS, far_loop, 0)
+    far_done(GROUPS - 1)
+
+    def near_step(th, c, first):
+        for kv in range(2):
+            total = near[th, kv] if not first else None
+            for k in range(blocks):
+                at = slice(k * half + c * chunk, k * half + (c + 1) * chunk)
+                product = jnp.dot(xflat[th, :, at], wbuf[0, kv, at, :], preferred_element_type=jnp.float32)
+                total = product if total is None else total + product
+            near[th, kv] = total
+
+    near_swap = remote(near.at[nf], near_peer, near_send.at[0], near_recv.at[0], partner)
+    for c in range(W_CHUNKS):
+        w_arrived(0, rd, c)
+        last = c == W_CHUNKS - 1
+
+        def both(i, carry):
+            th = jnp.where(i == 0, nf, f)
+            near_step(th, c, c == 0)
+            if last:
+                @pl.when(i == 0)
+                def _():
+                    near_swap.start()
+
             return carry
 
-        lax.fori_loop(0, 4, flatten, 0, unroll=True)
-
-        def one_side(kv, carry):
-            acc[th, kv] += jnp.dot(xflat[...], wbuf[z, kv], preferred_element_type=jnp.float32)
-            return carry
-
-        lax.fori_loop(0, 2, one_side, 0, unroll=True)
-
+        lax.fori_loop(0, 2, both, 0)
+
+    for i in range(len(order)):
+        grad_copy(i).wait_send()
     for c in range(W_CHUNKS):
-        w_arrived(rd, c)
-
-    def step(j, carry):
-        k = j // 2
-        th = nf + lax.rem(j, 2) * (1 - 2 * nf)
-
-        def side(s, inner):
-            z = t + (2 * s - 1) * k
-
-            @pl.when((z >= 0) & (z < n_tp))
-            def _():
-                @pl.when(k == n_tp - 1)
-                def _():
-                    x_arrived(z, th)
-
-                multiply(z, th)
-
-            return inner
-
-        lax.fori_loop(jnp.where(k == 0, 1, 0), 2, side, 0)
-        return carry
-
-    lax.fori_loop(0, 2 * n_tp - 1, step, 0)
-
-    swap = remote(acc.at[nf], partner_acc, acc_send.at[0], acc_recv.at[0], partner)
-    swap.start()
-    step(2 * n_tp - 1, 0)
-    for c in range(W_CHUNKS):
-        grad_copy(c).wait_send()
-        w_copy(c, 0).wait_send()
-        w_copy(c, 1).wait_send()
-        w_forward(c).wait_send()
-    x_swap.wait_send()
-    both_ways(lambda side: x_own(side).wait_send())
-    both_ways(lambda side: x_move(t, nf, side).wait_send())
-    for k in range(1, n_tp - 1):
-        for th in (f, nf):
-            @pl.when((t - k >= 0) & (t < n_tp - 1))
-            def _():
-                x_move(t - k, th, 1).wait_send()
-
-            @pl.when((t + k < n_tp) & (t > 0))
-            def _():
-                x_move(t + k, th, 0).wait_send()
+        w_pair(c).wait_send()
+        for cg in range(2):
+            w_copy(cg, c, 0).wait_send()
+            w_copy(cg, c, 1).wait_send()
+            w_forward(cg, c).wait_send()
+    for g in range(GROUPS):
+        x_swap(g).wait_send()
+        for h in range(2):
+            x_pair(g, h).wait_send()
+            x_mirror(g, h).wait_send()
+        far_swap(g).wait_send()
+        far_back(g).wait_send()
+
+    @pl.when(middle)
+    def _():
+        for g in range(GROUPS):
+            for h in range(2):
+                x_pair_mirror(g, h).wait_send()
+                x_relay(g, h).wait_send()
+
     for copy in outs:
         copy.wait()
     cached_copy.wait()
-    swap.wait_recv()
-    fresh_out[...] = (acc[f] + partner_acc[...]).astype(jnp.bfloat16)
-    swap.wait_send()
+    for g in range(GROUPS):
+        far_back(g).wait_recv()
+    near_swap.wait_recv()
+    fresh_out[...] = (near[f] + near_peer[...] + far_in[...]).astype(jnp.bfloat16)
+    near_swap.wait_send()
 
 
 def tail_kernel(
@@ -406,8 +489,9 @@
         pltpu.with_memory_space_constraint(array, pltpu.HBM)
         for array in (grad_parts, master_weight, moment_one, moment_two, layer_inputs, kv_cache)
     ]
+    half = depth // 2
     fresh, cached, master, one, two = pl.pallas_call(
-        functools.partial(learner_kernel, (n_tp, depth)),
+        learner_kernel,
         out_shape=(
             jax.ShapeDtypeStruct((2, tokens, width), bf16),
             jax.ShapeDtypeStruct((2, row_count * cache_len, width), bf16),
@@ -423,23 +507,36 @@
             pltpu.VMEM((2, depth, width), f32),
             pltpu.VMEM((2, depth, width), f32),
             pltpu.VMEM((2, depth, width), f32),
-            pltpu.VMEM((n_rep, 2, depth, width), bf16),
-            pltpu.VMEM((n_tp, 2, row_count, step_count, depth), bf16),
-            pltpu.VMEM((tokens, depth), bf16),
+            pltpu.VMEM((2, half, width), bf16),
+            pltpu.VMEM((2, 2, n_rep * half, width), bf16),
+            pltpu.VMEM((n_tp, 2, row_count, step_count, half), bf16),
+            pltpu.VMEM((2, tokens, n_tp * half), bf16),
+            pltpu.VMEM((2, 2, tokens, width), f32),
+            pltpu.VMEM((2, tokens, width), f32),
+            pltpu.VMEM((2, tokens, width), f32),
+            pltpu.VMEM((2, tokens, width), f32),
             pltpu.VMEM((2, 2, tokens, width), f32),
             pltpu.VMEM((2, tokens, width), f32),
             pltpu.VMEM(kv_cache.shape, bf16),
             pltpu.VMEM((2, row_count * cache_len, width), bf16),
-            dma((6,)),
+            dma((2 * W_CHUNKS,)),
+            dma((3, 2 * W_CHUNKS)),
+            dma((1,)),
+            dma((1,)),
             dma((4,)),
+            dma((2 * W_CHUNKS,)),
+            dma((2 * W_CHUNKS,)),
+            dma((9, GROUPS)),
+            dma((n_tp, 2, GROUPS)),
             dma((W_CHUNKS,)),
             dma((W_CHUNKS,)),
-            dma((2, n_tp, 2)),
-            dma((n_tp, 2)),
-            dma((1,)),
+            dma((2, 2, W_CHUNKS)),
+            dma((2, n_rep, W_CHUNKS)),
             dma((2, W_CHUNKS)),
-            dma((n_rep, W_CHUNKS)),
-            dma((W_CHUNKS,)),
+            dma((GROUPS,)),
+            dma((GROUPS,)),
+            dma((GROUPS,)),
+            dma((GROUPS,)),
             dma((1,)),
             dma((1,)),
         ],

time: 62.3 us -> 74.1 us (1.19)
  Pallas kernels: 61.5 us -> 73.3 us
    pallas_call x1, Pallas kernels: 57 us -> 68.8 us  [fused_device(): pl.pallas_call(learner_kernel, out_shape=(jax.ShapeDtypeStruct((2, tokens...]
where the time goes in v1:
time: 74.1 us; the launch traced here: 73.9 us
  Pallas kernels  73.3 us (99%)
    pallas_call x1, Pallas kernels, fused_device(): pl.pallas_call(learner_kernel, out_shape=(jax.ShapeDtypeStruct((2, tokens...  68.8 us
    pallas_call x1, Pallas kernels, fused_device(): pl.pallas_call(tail_kernel, out_shape=(jax.ShapeDtypeStruct(queries.shape...  4.42 us

profile of v1, /device:TPU:0, one launch (start us, length us, event | category | flops | bytes accessed | tf_op | source)
XLA Modules:
  0.0 73.9 jit_solution(9225873072033442305)
XLA Ops:
  0.6 0.0 copy-start.1
  0.6 0.0 copy-start
  0.7 68.8 %shard_map.111 = (bf16[2,192,256]{2,1,0:T(8,128)(2,1)S(1)}, bf16[2,1152,256]{2,1,0:T(8,128)(2,1)S(1)}, f32[2,1024,256]{2,1,0:T(8,128)S(1)}, f32[2,1024,256]{2,1,0:T(8,128)S(1)}, f32[2,1024,256]{2,1,0:T(8,128)S(1)}) custom-call(bf16[1,2,2048,256]{3,2,1,0:T(8,128)(2,1)} %grad_hbm.1, f32[2,1024,256]{2,1,0:T(8,128)} %master_hbm.1, f32[2,1024,256]{2,1,0:T(8,128)} %one_hbm.1, ...), custom_call_target="tpu_custom_call" | custom-call | tf_op jit(solution)/shard_map/pallas_call | solution.py:493
  69.5 0.0 copy-done.1
  69.5 0.0 copy-done
  69.5 4.4 %shard_map.112 = (bf16[48,4,2048]{2,1,0:T(4,128)(2,1)}, f32[2,1024,256]{2,1,0:T(8,128)}, f32[2,1024,256]{2,1,0:T(8,128)}, f32[2,1024,256]{2,1,0:T(8,128)}) custom-call(s32[48]{0:T(128)S(1)} %copy-done.1, bf16[48,4,2048]{2,1,0:T(4,128)(2,1)S(1)} %copy-done, bf16[2,1152,256]{2,1,0:T(8,128)(2,1)S(1)} %get-tuple-element.13.kv_ref, ...), custom_call_target="tpu_custom_call" | custom-call | tf_op jit(solution)/shard_map/pallas_call | solution.py:549
Async XLA Ops:
  0.6 68.9 %copy-start.1 = (s32[48]{0:T(128)S(1)}, s32[48]{0:T(128)}, u32[]{:S(2)}) copy-start(s32[48]{0:T(128)} %lengths.1) | copy-start | bytes 580
  0.6 68.9 %copy-start = (bf16[48,4,2048]{2,1,0:T(4,128)(2,1)S(1)}, bf16[48,4,2048]{2,1,0:T(4,128)(2,1)}, u32[]{:S(2)}) copy-start(bf16[48,4,2048]{2,1,0:T(4,128)(2,1)} %q_ref.1) | copy-start | bytes 2359300

commit v2 on v1

--- a/solution.py
+++ b/solution.py
@@ -9,7 +9,8 @@
 
 HD = 128
 MESH = pl.DeviceIdType.MESH
-W_CHUNKS = 2
+W_CHUNKS = 4
+W_EARLY = 2
 GROUPS = 4
 ADAM_SUB = 32
 TAIL_ROWS = 8
@@ -136,25 +137,21 @@
             x_send.at[0, g], x_recv.at[k, th, g], partner,
         ).wait_recv()
 
-    def x_out(g):
-        for h in range(2):
-            x_pair(g, h).start()
-        for h in range(2):
-            x_mirror(g, h).start()
-
-        @pl.when(middle)
-        def _():
+    def go(make, groups):
+        for g in groups:
             for h in range(2):
-                x_pair_mirror(g, h).start()
+                make(g, h).start()
+
+    every = range(GROUPS)
+    early = range(GROUPS // 2)
+    late = range(GROUPS // 2, GROUPS)
 
     def relay(g):
         for th in range(2):
             x_arrived(pair, th, g)
 
-        @pl.when(middle)
-        def _():
-            for th in range(2):
-                x_relay(g, th).start()
+        for th in range(2):
+            x_relay(g, th).start()
 
     def w_pair(c):
         return remote(
@@ -195,7 +192,16 @@
         w_go(1, c)
 
     grad_copy(0).start()
-    x_out(0)
+
+    @pl.when(middle)
+    def _():
+        go(x_mirror, every)
+        go(x_pair, early)
+
+    @pl.when(jnp.logical_not(middle))
+    def _():
+        go(x_pair, early)
+
     for i in range(1, len(order)):
         grad_copy(i).start()
     for g in range(GROUPS):
@@ -232,10 +238,9 @@
             w_pair(c).start()
         else:
             adam(sub, c, wbuf.at[0], r * half)
-            if c < W_CHUNKS // 2:
+            if c < W_EARLY:
                 w_go(0, c)
-    for g in range(1, GROUPS):
-        x_out(g)
+
     outs = [
         pltpu.make_async_copy(master, master_out, out_sem.at[0]),
         pltpu.make_async_copy(one, one_out, out_sem.at[1]),
@@ -259,28 +264,54 @@
 
         lax.fori_loop(0, pieces, body, 0)
 
-    relay(0)
-    split_cache(0)
-    split_cache(1)
-    for c in range(W_CHUNKS // 2):
-        w_step(0, c)
-    for c in range(W_CHUNKS):
-        pair_step(c)
-    for c in range(W_CHUNKS // 2, W_CHUNKS):
-        w_go(0, c)
-    relay(1)
-    split_cache(2)
-    split_cache(3)
+    @pl.when(middle)
+    def _():
+        for g in early:
+            relay(g)
+
+    @pl.when(jnp.logical_not(middle))
+    def _():
+        go(x_pair, late)
+
+    def send_next(item):
+        cg, c = item
+        if cg == 1:
+            pair_step(c)
+        else:
+            w_go(0, c)
+
+    items = [(0, c) for c in range(W_EARLY)] + [(1, c) for c in range(W_CHUNKS)]
+    items += [(0, c) for c in range(W_EARLY, W_CHUNKS)]
+    for i in range(W_EARLY + W_CHUNKS):
+        w_step(*items[i])
+        if i + W_EARLY < len(items):
+            send_next(items[i + W_EARLY])
+            if items[i + W_EARLY] == (1, W_CHUNKS - 1):
+                @pl.when(middle)
+                def _():
+                    go(x_pair, late)
+                    go(x_pair_mirror, early)
+
+                @pl.when(jnp.logical_not(middle))
+                def _():
+                    go(x_mirror, every)
+
+        if i < 4:
+            split_cache(i)
+        if i == W_CHUNKS:
+            @pl.when(middle)
+            def _():
+                for g in late:
+                    relay(g)
+                go(x_pair_mirror, late)
     cached_copy = pltpu.make_async_copy(kv_flat, cached_out, out_sem.at[3])
     cached_copy.start()
-    for c in range(W_CHUNKS // 2):
-        w_step(1, c)
-    relay(2)
-    for c in range(W_CHUNKS // 2, W_CHUNKS):
-        w_step(1, c)
-    relay(3)
     for c in range(W_CHUNKS):
         w_arrived(1, rd, c)
+    for c in range(W_EARLY):
+        w_arrived(0, rd, c)
+    for c in range(W_EARLY, W_CHUNKS - 1):
+        w_step(0, c)
 
     def far_swap(g):
         return remote(
@@ -292,7 +323,20 @@
             far_out.at[:, tokens(g), :], far_in.at[:, tokens(g), :], back_send.at[g], back_recv.at[g], (r, f, pair)
         )
 
+    def near_part(lhs, kv, start, stop):
+        total = None
+        for k in range(blocks):
+            at = slice(k * half + start * chunk, k * half + stop * chunk)
+            product = jnp.dot(lhs[:, at], wbuf[0, kv, at, :], preferred_element_type=jnp.float32)
+            total = product if total is None else total + product
+        return total
+
     def far_step(g, carry):
+        @pl.when(jnp.logical_not(middle))
+        def _():
+            for th in range(2):
+                x_arrived(pair, th, g)
+
         x_arrived(t, nf, g)
         for th in range(2):
             x_arrived(mirror, th, g)
@@ -311,11 +355,16 @@
             for th in range(2):
                 far[th, kv, tokens(g), :] = product[th * group_tokens : (th + 1) * group_tokens]
         far_swap(g).start()
+        for kv in range(2):
+            product = near_part(lhs, kv, 0, W_EARLY)
+            for th in range(2):
+                near[th, kv, tokens(g), :] = product[th * group_tokens : (th + 1) * group_tokens]
         return carry
 
     def far_done(g):
         far_swap(g).wait_recv()
-        far_out[:, tokens(g), :] = far[f, :, tokens(g), :] + far_peer[:, tokens(g), :]
+        both = far[f, :, tokens(g), :] + far_peer[:, tokens(g), :]
+        far_out[:, tokens(g), :] = both.astype(jnp.bfloat16)
         far_back(g).start()
 
     def far_loop(g, carry):
@@ -325,41 +374,31 @@
         def _():
             far_done(g - 1)
 
-        @pl.when(g == 1)
+        @pl.when(g == 0)
         def _():
-            for c in range(W_CHUNKS // 2, W_CHUNKS):
-                w_step(0, c)
+            w_step(0, W_CHUNKS - 1)
 
         return carry
 
     lax.fori_loop(0, GROUPS, far_loop, 0)
     far_done(GROUPS - 1)
 
-    def near_step(th, c, first):
+    near_swap = remote(near.at[nf], near_peer, near_send.at[0], near_recv.at[0], partner)
+    for c in range(W_EARLY, W_CHUNKS):
+        w_arrived(0, rd, c)
+
+    def near_last(i, carry):
+        th = jnp.where(i == 0, nf, f)
         for kv in range(2):
-            total = near[th, kv] if not first else None
-            for k in range(blocks):
-                at = slice(k * half + c * chunk, k * half + (c + 1) * chunk)
-                product = jnp.dot(xflat[th, :, at], wbuf[0, kv, at, :], preferred_element_type=jnp.float32)
-                total = product if total is None else total + product
-            near[th, kv] = total
-
-    near_swap = remote(near.at[nf], near_peer, near_send.at[0], near_recv.at[0], partner)
-    for c in range(W_CHUNKS):
-        w_arrived(0, rd, c)
-        last = c == W_CHUNKS - 1
-
-        def both(i, carry):
-            th = jnp.where(i == 0, nf, f)
-            near_step(th, c, c == 0)
-            if last:
-                @pl.when(i == 0)
-                def _():
-                    near_swap.start()
-
-            return carry
-
-        lax.fori_loop(0, 2, both, 0)
+            near[th, kv] += near_part(xflat.at[th], kv, W_EARLY, W_CHUNKS)
+
+        @pl.when(i == 0)
+        def _():
+            near_swap.start()
+
+        return carry
+
+    lax.fori_loop(0, 2, near_last, 0)
 
     for i in range(len(order)):
         grad_copy(i).wait_send()
@@ -390,7 +429,7 @@
     for g in range(GROUPS):
         far_back(g).wait_recv()
     near_swap.wait_recv()
-    fresh_out[...] = (near[f] + near_peer[...] + far_in[...]).astype(jnp.bfloat16)
+    fresh_out[...] = (near[f] + near_peer[...] + far_in[...].astype(jnp.float32)).astype(jnp.bfloat16)
     near_swap.wait_send()
 
 
@@ -513,8 +552,8 @@
             pltpu.VMEM((2, tokens, n_tp * half), bf16),
             pltpu.VMEM((2, 2, tokens, width), f32),
             pltpu.VMEM((2, tokens, width), f32),
-            pltpu.VMEM((2, tokens, width), f32),
-            pltpu.VMEM((2, tokens, width), f32),
+            pltpu.VMEM((2, tokens, width), bf16),
+            pltpu.VMEM((2, tokens, width), bf16),
             pltpu.VMEM((2, 2, tokens, width), f32),
             pltpu.VMEM((2, tokens, width), f32),
             pltpu.VMEM(kv_cache.shape, bf16),

time: 74.1 us -> 57.6 us (0.78)
  Pallas kernels: 73.3 us -> 56.7 us
    pallas_call x1, Pallas kernels: 68.8 us -> 52.3 us  [fused_device(): pl.pallas_call(learner_kernel, out_shape=(jax.ShapeDtypeStruct((2, tokens...]
where the time goes in v2:
time: 57.6 us; the launch traced here: 57.4 us
  Pallas kernels  56.7 us (98%)
  between operations  0.67 us (1%)
    pallas_call x1, Pallas kernels, fused_device(): pl.pallas_call(learner_kernel, out_shape=(jax.ShapeDtypeStruct((2, tokens...  52.3 us
    pallas_call x1, Pallas kernels, fused_device(): pl.pallas_call(tail_kernel, out_shape=(jax.ShapeDtypeStruct(queries.shape...  4.42 us

profile of v2, /device:TPU:0, one launch (start us, length us, event | category | flops | bytes accessed | tf_op | source)
XLA Modules:
  0.0 57.4 jit_solution(12588599732255961750)
XLA Ops:
  0.6 0.0 copy-start.1
  0.6 0.0 copy-start
  0.7 52.3 %shard_map.111 = (bf16[2,192,256]{2,1,0:T(8,128)(2,1)S(1)}, bf16[2,1152,256]{2,1,0:T(8,128)(2,1)S(1)}, f32[2,1024,256]{2,1,0:T(8,128)S(1)}, f32[2,1024,256]{2,1,0:T(8,128)S(1)}, f32[2,1024,256]{2,1,0:T(8,128)S(1)}) custom-call(bf16[1,2,2048,256]{3,2,1,0:T(8,128)(2,1)} %grad_hbm.1, f32[2,1024,256]{2,1,0:T(8,128)} %master_hbm.1, f32[2,1024,256]{2,1,0:T(8,128)} %one_hbm.1, ...), custom_call_target="tpu_custom_call" | custom-call | tf_op jit(solution)/shard_map/pallas_call | solution.py:532
  53.0 0.0 copy-done.1
  53.0 0.0 copy-done
  53.0 4.4 %shard_map.112 = (bf16[48,4,2048]{2,1,0:T(4,128)(2,1)}, f32[2,1024,256]{2,1,0:T(8,128)}, f32[2,1024,256]{2,1,0:T(8,128)}, f32[2,1024,256]{2,1,0:T(8,128)}) custom-call(s32[48]{0:T(128)S(1)} %copy-done.1, bf16[48,4,2048]{2,1,0:T(4,128)(2,1)S(1)} %copy-done, bf16[2,1152,256]{2,1,0:T(8,128)(2,1)S(1)} %get-tuple-element.13.kv_ref, ...), custom_call_target="tpu_custom_call" | custom-call | tf_op jit(solution)/shard_map/pallas_call | solution.py:588
Async XLA Ops:
  0.6 52.3 %copy-start.1 = (s32[48]{0:T(128)S(1)}, s32[48]{0:T(128)}, u32[]{:S(2)}) copy-start(s32[48]{0:T(128)} %lengths.1) | copy-start | bytes 580
  0.6 52.3 %copy-start = (bf16[48,4,2048]{2,1,0:T(4,128)(2,1)S(1)}, bf16[48,4,2048]{2,1,0:T(4,128)(2,1)}, u32[]{:S(2)}) copy-start(bf16[48,4,2048]{2,1,0:T(4,128)(2,1)} %q_ref.1) | copy-start | bytes 2359300

commit v3 on v2

--- a/solution.py
+++ b/solution.py
@@ -14,16 +14,16 @@
 GROUPS = 4
 ADAM_SUB = 32
 TAIL_ROWS = 8
-TAIL_BLOCKS = 3
 LOG2E = 1.4426950408889634
+LOW = -0.7 * 3.4028234663852886e38
 
 
 def learner_kernel(
-    grad_hbm, master_hbm, one_hbm, two_hbm, x_hbm, kv_hbm,
-    fresh_out, cached_out, master_out, one_out, two_out,
+    lengths_hbm, grad_hbm, master_hbm, one_hbm, two_hbm, x_hbm, kv_hbm, q_hbm,
+    fresh_out, query_out, old_out, mass_out, master_out, one_out, two_out,
     own_grad, peer_grad, master, one, two, wpair, wbuf, xbuf, xflat,
-    far, far_peer, far_out, far_in, near, near_peer, kv_raw, kv_flat,
-    grad_sem, state_sem, x_sem, kv_sem, out_sem, grad_send, grad_recv, x_send, x_recv,
+    far, far_peer, far_out, far_in, near, near_peer, kv_raw, q_raw, lengths, xstage,
+    grad_sem, state_sem, x_sem, kv_sem, out_sem, grad_send, grad_recv, x_send, x_recv, stage_send, stage_recv,
     pair_send, pair_recv, w_send, w_recv, w_fwd_send, far_send, far_recv, back_send, back_recv, near_send, near_recv,
 ):
     r, f, t = lax.axis_index("rep"), lax.axis_index("fsdp"), lax.axis_index("tp")
@@ -83,6 +83,10 @@
     kv_local = pltpu.make_async_copy(kv_hbm, kv_raw, kv_sem.at[0])
     x_local.start()
     kv_local.start()
+    q_local = pltpu.make_async_copy(q_hbm, q_raw, kv_sem.at[1])
+    q_local.start()
+    length_local = pltpu.make_async_copy(lengths_hbm, lengths, kv_sem.at[2])
+    length_local.start()
 
     barrier = pltpu.get_barrier_semaphore()
     friends = [partner, dev_x, dev_y]
@@ -131,6 +135,26 @@
             x_send.at[7 + th, g], x_recv.at[pair, th, g], (r, f, mirror),
         )
 
+    def x_stage(g, h):
+        return remote(
+            x_hbm.at[some_rows(g), :, features(h, theirs)], xstage.at[f, some_rows(g)],
+            x_send.at[5 + h, g], stage_recv.at[f, g], (r, h, mirror),
+        )
+
+    def x_unstage(g, th):
+        return remote(
+            xstage.at[th, some_rows(g)], xbuf.at[mirror, th, some_rows(g)],
+            stage_send.at[th, g], x_recv.at[mirror, th, g], (r, f, pair),
+        )
+
+    def unstage(g):
+        for th in range(2):
+            remote(
+                xstage.at[th, some_rows(g)], xstage.at[th, some_rows(g)],
+                x_send.at[5, g], stage_recv.at[th, g], (r, f, mirror),
+            ).wait_recv()
+            x_unstage(g, th).start()
+
     def x_arrived(k, th, g):
         remote(
             xbuf.at[k, th, some_rows(g)], xbuf.at[k, th, some_rows(g)],
@@ -195,8 +219,9 @@
 
     @pl.when(middle)
     def _():
+        go(x_pair, [0])
         go(x_mirror, every)
-        go(x_pair, early)
+        go(x_stage, early)
 
     @pl.when(jnp.logical_not(middle))
     def _():
@@ -250,19 +275,52 @@
         copy.start()
     x_local.wait()
     kv_local.wait()
+    q_local.wait()
+    length_local.wait()
 
     kv_rows, cache_len = kv_raw.shape[:2]
-    pieces = kv_rows // 8
-
-    def split_cache(quarter):
-        def body(i, carry):
-            row = (quarter * pieces + i) * 2
-            at = pl.ds(pl.multiple_of(row * cache_len, 2 * cache_len), 2 * cache_len)
-            for j in range(2):
-                kv_flat[j, at, :] = kv_raw[pl.ds(row, 2), :, j, :].reshape(2 * cache_len, -1)
-            return carry
-
-        lax.fori_loop(0, pieces, body, 0)
+    parts = kv_rows // TAIL_ROWS
+    head = HD
+    groups = kv_raw.shape[3] // head
+    per_group = q_raw.shape[2] // head // groups
+    part_tokens = TAIL_ROWS * x_steps
+    keys = TAIL_ROWS * cache_len
+    column = lax.broadcasted_iota(jnp.int32, (1, keys), 1)
+    key_row = column // cache_len
+    position = column - key_row * cache_len
+    token_row = lax.broadcasted_iota(jnp.int32, (part_tokens, 1), 0) // x_steps
+    factor = head**-0.5 * LOG2E
+
+    def cached_part(part):
+        mine_rows = slice(part * TAIL_ROWS, (part + 1) * TAIL_ROWS)
+        limit = jnp.zeros((1, keys), jnp.int32)
+        for at in range(TAIL_ROWS):
+            limit = jnp.where(key_row == at, lengths[part * TAIL_ROWS + at], limit)
+        valid = jnp.where(position < limit, key_row, -1) == token_row
+        for group in range(groups):
+            cols = slice(group * head, (group + 1) * head)
+            query = jnp.concatenate(
+                [
+                    q_raw[mine_rows, :, (group * per_group + h) * head : (group * per_group + h + 1) * head].reshape(
+                        part_tokens, head
+                    )
+                    for h in range(per_group)
+                ],
+                axis=0,
+            )
+            key = kv_raw[mine_rows, :, 0, cols].reshape(keys, head)
+            value = kv_raw[mine_rows, :, 1, cols].reshape(keys, head)
+            scores = lax.dot_general(query, key, (((1,), (1,)), ((), ())), preferred_element_type=jnp.float32)
+            scores = jnp.where(valid[None], scores.reshape(per_group, part_tokens, keys), LOW)
+            scores = scores.reshape(per_group * part_tokens, keys)
+            top = jnp.max(scores, axis=-1, keepdims=True)
+            weights = jnp.exp2((scores - top) * factor)
+            total = jnp.sum(weights, axis=-1, keepdims=True)
+            old = jnp.dot(weights.astype(jnp.bfloat16), value, preferred_element_type=jnp.float32)
+            where = part * groups + group
+            query_out[where] = query
+            old_out[where] = old * (1.0 / total)
+            mass_out[where] = jnp.broadcast_to(top + jnp.log2(total) * (1.0 / factor), old.shape)
 
     @pl.when(middle)
     def _():
@@ -286,26 +344,40 @@
         w_step(*items[i])
         if i + W_EARLY < len(items):
             send_next(items[i + W_EARLY])
+            if items[i + W_EARLY] == (1, W_CHUNKS - 3):
+                @pl.when(middle)
+                def _():
+                    go(x_pair, every[1:])
+
+            if items[i + W_EARLY] == (1, W_CHUNKS - 2):
+                @pl.when(middle)
+                def _():
+                    for g in early:
+                        unstage(g)
+
+                @pl.when(jnp.logical_not(middle))
+                def _():
+                    go(x_mirror, early)
+
             if items[i + W_EARLY] == (1, W_CHUNKS - 1):
                 @pl.when(middle)
                 def _():
-                    go(x_pair, late)
-                    go(x_pair_mirror, early)
+                    for g in late:
+                        relay(g)
+
+            if items[i + W_EARLY] == (0, W_EARLY):
+                @pl.when(middle)
+                def _():
+                    go(x_pair_mirror, late)
 
                 @pl.when(jnp.logical_not(middle))
                 def _():
-                    go(x_mirror, every)
-
-        if i < 4:
-            split_cache(i)
-        if i == W_CHUNKS:
-            @pl.when(middle)
-            def _():
-                for g in late:
-                    relay(g)
-                go(x_pair_mirror, late)
-    cached_copy = pltpu.make_async_copy(kv_flat, cached_out, out_sem.at[3])
-    cached_copy.start()
+                    go(x_mirror, late)
+
+        if i < parts:
+            cached_part(i)
+    for part in range(W_EARLY + W_CHUNKS, parts):
+        cached_part(part)
     for c in range(W_CHUNKS):
         w_arrived(1, rd, c)
     for c in range(W_EARLY):
@@ -418,14 +490,17 @@
 
     @pl.when(middle)
     def _():
-        for g in range(GROUPS):
-            for h in range(2):
+        for h in range(2):
+            for g in every:
+                x_relay(g, h).wait_send()
+            for g in early:
+                x_stage(g, h).wait_send()
+                x_unstage(g, h).wait_send()
+            for g in late:
                 x_pair_mirror(g, h).wait_send()
-                x_relay(g, h).wait_send()
 
     for copy in outs:
         copy.wait()
-    cached_copy.wait()
     for g in range(GROUPS):
         far_back(g).wait_recv()
     near_swap.wait_recv()
@@ -434,83 +509,55 @@
 
 
 def tail_kernel(
-    lengths, q_ref, kv_ref, fresh_in, master_in, one_in, two_in,
-    context, master_out, one_out, two_out, fresh_ref, sem,
+    query_ref, old_ref, mass_ref, fresh_ref, master_in, one_in, two_in,
+    context, master_out, one_out, two_out, out_ref, sem,
 ):
-    block = pl.program_id(0)
     moves = [
-        pltpu.make_async_copy(master_in, master_out, sem.at[1]),
-        pltpu.make_async_copy(one_in, one_out, sem.at[2]),
-        pltpu.make_async_copy(two_in, two_out, sem.at[3]),
+        pltpu.make_async_copy(source.at[kv], target.at[kv], sem.at[2 * i + kv])
+        for i, (source, target) in enumerate(((master_in, master_out), (one_in, one_out), (two_in, two_out)))
+        for kv in range(2)
     ]
-
-    @pl.when(block == 0)
-    def _():
-        fresh_copy = pltpu.make_async_copy(fresh_in, fresh_ref, sem.at[0])
-        fresh_copy.start()
-        for move in moves:
-            move.start()
-        fresh_copy.wait()
-
-    step_rows, step_count, features = q_ref.shape
-    row_count = TAIL_ROWS
+    for move in moves:
+        move.start()
+    row_count, step_count, features = out_ref.shape
     head = HD
-    cache_len = kv_ref.shape[1] // step_rows
-    cached = row_count * cache_len
-    tokens = row_count * step_count
-    keys = cached + tokens
     groups = fresh_ref.shape[2] // head
     per_group = features // head // groups
-    column = lax.broadcasted_iota(jnp.int32, (1, keys), 1)
-    is_old = column < cached
-    new_column = column - cached
-    key_row = jnp.where(is_old, column // cache_len, new_column // step_count)
-    position = column - key_row * cache_len
-    new_row = jnp.where(is_old, -1, key_row)
+    tokens = TAIL_ROWS * step_count
+    parts = row_count // TAIL_ROWS
     token = lax.broadcasted_iota(jnp.int32, (tokens, 1), 0)
-    row = token // step_count
-    new_valid = (new_row == row) & (new_column <= token)
-    low = -0.7 * float(jnp.finfo(jnp.float32).max)
+    column = lax.broadcasted_iota(jnp.int32, (1, tokens), 1)
+    valid = (column // step_count == token // step_count) & (column <= token)
     factor = head**-0.5 * LOG2E
     contract = (((1,), (1,)), ((), ()))
-    for part in range(step_rows // row_count):
-        first_row = part * row_count
-        start = block * step_rows + first_row
-        limit = jnp.zeros((1, keys), jnp.int32)
-        for at in range(row_count):
-            limit = jnp.where(key_row == at, lengths[start + at], limit)
-        valid = (jnp.where(is_old & (position < limit), key_row, -1) == row) | new_valid
-        here = pl.ds(pl.multiple_of(start * step_count, tokens), tokens)
-        old = slice(first_row * cache_len, first_row * cache_len + cached)
-        mine = slice(first_row, first_row + row_count)
+    writes = []
+    for part in range(parts):
+        here = slice(part * tokens, (part + 1) * tokens)
+        mine = slice(part * TAIL_ROWS, (part + 1) * TAIL_ROWS)
         for group in range(groups):
             cols = slice(group * head, (group + 1) * head)
-            query = jnp.concatenate(
-                [
-                    q_ref[mine, :, (group * per_group + h) * head : (group * per_group + h + 1) * head].reshape(
-                        tokens, head
-                    )
-                    for h in range(per_group)
-                ],
-                axis=0,
+            where = part * groups + group
+            scores = lax.dot_general(
+                query_ref[where], fresh_ref[0, here, cols], contract, preferred_element_type=jnp.float32
             )
-            key = jnp.concatenate([kv_ref[0, old, cols], fresh_ref[0, here, cols]], axis=0)
-            value = jnp.concatenate([kv_ref[1, old, cols], fresh_ref[1, here, cols]], axis=0)
-            scores = lax.dot_general(query, key, contract, preferred_element_type=jnp.float32)
-            scores = jnp.where(valid[None], scores.reshape(per_group, tokens, keys), low)
-            weights = jnp.exp2((scores - jnp.max(scores, axis=-1, keepdims=True)) * factor)
-            weights = weights * (1.0 / jnp.sum(weights, axis=-1, keepdims=True))
-            weights = weights.astype(jnp.bfloat16).reshape(per_group * tokens, keys)
-            out = jnp.dot(weights, value, preferred_element_type=jnp.float32)
+            scores = jnp.where(valid[None], scores.reshape(per_group, tokens, tokens), LOW)
+            scores = scores.reshape(per_group * tokens, tokens)
+            mass = mass_ref[where]
+            top = jnp.maximum(mass, jnp.max(scores, axis=-1, keepdims=True))
+            old_weight = jnp.exp2((mass - top) * factor)
+            weights = jnp.exp2((scores - top[:, :tokens]) * factor)
+            scale = 1.0 / (old_weight + jnp.sum(weights, axis=-1, keepdims=True))
+            new = jnp.dot(weights.astype(jnp.bfloat16), fresh_ref[1, here, cols], preferred_element_type=jnp.float32)
+            out = (old_weight * old_ref[where] + new) * scale
             for h in range(per_group):
                 at = (group * per_group + h) * head
-                piece = out[h * tokens : (h + 1) * tokens].reshape(row_count, step_count, head)
-                context[mine, :, at : at + head] = piece.astype(jnp.bfloat16)
-
-    @pl.when(block == pl.num_programs(0) - 1)
-    def _():
-        for move in moves:
-            move.wait()
+                piece = out[h * tokens : (h + 1) * tokens].reshape(TAIL_ROWS, step_count, head)
+                out_ref[mine, :, at : at + head] = piece.astype(jnp.bfloat16)
+        write = pltpu.make_async_copy(out_ref.at[mine], context.at[mine], sem.at[6 + part])
+        write.start()
+        writes.append(write)
+    for write in writes + moves:
+        write.wait()
 
 
 def fused_device(n_rep, grad_parts, master_weight, moment_one, moment_two, layer_inputs, queries, kv_cache, lengths):
@@ -518,7 +565,6 @@
     _, depth, width = master_weight.shape
     n_tp = n_rep
     tokens = row_count * step_count
-    cache_len = kv_cache.shape[1]
     bf16, f32 = jnp.bfloat16, jnp.float32
     dma = pltpu.SemaphoreType.DMA
     state = jax.ShapeDtypeStruct(master_weight.shape, f32)
@@ -526,20 +572,26 @@
     hbm_spec = pl.BlockSpec(memory_space=pltpu.HBM)
     in_place = [
         pltpu.with_memory_space_constraint(array, pltpu.HBM)
-        for array in (grad_parts, master_weight, moment_one, moment_two, layer_inputs, kv_cache)
+        for array in (lengths, grad_parts, master_weight, moment_one, moment_two, layer_inputs, kv_cache, queries)
     ]
     half = depth // 2
-    fresh, cached, master, one, two = pl.pallas_call(
+    vmem_spec = pl.BlockSpec(memory_space=pltpu.VMEM)
+    parts = row_count // TAIL_ROWS
+    groups = width // HD
+    stacked = (parts * groups, queries.shape[2] // width * TAIL_ROWS * step_count, HD)
+    fresh, query, old, mass, master, one, two = pl.pallas_call(
         learner_kernel,
         out_shape=(
             jax.ShapeDtypeStruct((2, tokens, width), bf16),
-            jax.ShapeDtypeStruct((2, row_count * cache_len, width), bf16),
+            jax.ShapeDtypeStruct(stacked, bf16),
+            jax.ShapeDtypeStruct(stacked, f32),
+            jax.ShapeDtypeStruct(stacked, f32),
             state,
             state,
             state,
         ),
-        in_specs=[hbm_spec] * 6,
-        out_specs=(pl.BlockSpec(memory_space=pltpu.VMEM), hbm_spec, any_spec, any_spec, any_spec),
+        in_specs=[hbm_spec] * 8,
+        out_specs=(vmem_spec,) * 4 + (any_spec,) * 3,
         scratch_shapes=[
             pltpu.VMEM((2, depth, width), bf16),
             pltpu.VMEM((2, depth, width), bf16),
@@ -557,16 +609,20 @@
             pltpu.VMEM((2, 2, tokens, width), f32),
             pltpu.VMEM((2, tokens, width), f32),
             pltpu.VMEM(kv_cache.shape, bf16),
-            pltpu.VMEM((2, row_count * cache_len, width), bf16),
+            pltpu.VMEM(queries.shape, bf16),
+            pltpu.SMEM(lengths.shape, jnp.int32),
+            pltpu.VMEM((2, row_count, step_count, half), bf16),
             dma((2 * W_CHUNKS,)),
             dma((3, 2 * W_CHUNKS)),
             dma((1,)),
-            dma((1,)),
-            dma((4,)),
+            dma((3,)),
+            dma((3,)),
             dma((2 * W_CHUNKS,)),
             dma((2 * W_CHUNKS,)),
             dma((9, GROUPS)),
             dma((n_tp, 2, GROUPS)),
+            dma((2, GROUPS)),
+            dma((2, GROUPS)),
             dma((W_CHUNKS,)),
             dma((W_CHUNKS,)),
             dma((2, 2, W_CHUNKS)),
@@ -583,29 +639,14 @@
             collective_id=0, has_side_effects=True, vmem_limit_bytes=36 * 1024 * 1024
         ),
     )(*in_place)
-    step_rows = TAIL_ROWS * TAIL_BLOCKS
-    token_spec = pl.BlockSpec((step_rows, step_count, features), lambda i, *_: (i, 0, 0))
     context, master, one, two = pl.pallas_call(
         tail_kernel,
         out_shape=(jax.ShapeDtypeStruct(queries.shape, bf16), state, state, state),
-        grid_spec=pltpu.PrefetchScalarGridSpec(
-            num_scalar_prefetch=1,
-            grid=(row_count // step_rows,),
-            in_specs=[
-                token_spec,
-                pl.BlockSpec((2, step_rows * cache_len, width), lambda i, *_: (0, i, 0)),
-                any_spec,
-                any_spec,
-                any_spec,
-                any_spec,
-            ],
-            out_specs=(token_spec, hbm_spec, hbm_spec, hbm_spec),
-            scratch_shapes=[pltpu.VMEM((2, tokens, width), bf16), dma((4,))],
-        ),
-        compiler_params=pltpu.CompilerParams(
-            dimension_semantics=("arbitrary",), vmem_limit_bytes=16 * 1024 * 1024
-        ),
-    )(lengths, queries, cached, fresh, master, one, two)
+        in_specs=[vmem_spec] * 4 + [any_spec] * 3,
+        out_specs=(hbm_spec,) * 4,
+        scratch_shapes=[pltpu.VMEM(queries.shape, bf16), dma((6 + parts,))],
+        compiler_params=pltpu.CompilerParams(vmem_limit_bytes=16 * 1024 * 1024),
+    )(query, old, mass, fresh, master, one, two)
     return (master, one, two, context)
 
 

time: 57.6 us -> 54.7 us (0.950)
  Pallas kernels: 56.7 us -> 53.7 us
    pallas_call x1, Pallas kernels: 52.3 us -> 50.8 us  [fused_device(): pl.pallas_call(learner_kernel, out_shape=(jax.ShapeDtypeStruct((2, tokens...]
    pallas_call x1, Pallas kernels: 4.42 us -> 2.98 us  [fused_device(): pl.pallas_call(tail_kernel, out_shape=(jax.ShapeDtypeStruct(queries.shape...]
where the time goes in v3:
time: 54.7 us; the launch traced here: 54.4 us
  Pallas kernels  53.7 us (98%)
  between operations  0.64 us (1%)
    pallas_call x1, Pallas kernels, fused_device(): pl.pallas_call(learner_kernel, out_shape=(jax.ShapeDtypeStruct((2, tokens...  50.8 us
    pallas_call x1, Pallas kernels, fused_device(): pl.pallas_call(tail_kernel, out_shape=(jax.ShapeDtypeStruct(queries.shape...  2.98 us

profile of v3, /device:TPU:0, one launch (start us, length us, event | category | flops | bytes accessed | tf_op | source)
XLA Modules:
  0.0 54.4 jit_solution(1450585156256538518)
XLA Ops:
  0.6 50.8 %shard_map.111 = (bf16[2,192,256]{2,1,0:T(8,128)(2,1)S(1)}, bf16[12,256,128]{2,1,0:T(8,128)(2,1)S(1)}, f32[12,256,128]{2,1,0:T(8,128)S(1)}, f32[12,256,128]{2,1,...) custom-call(s32[48]{0:T(128)} %lengths_hbm.1, ...), custom_call_target="tpu_custom_call" | custom-call | tf_op jit(solution)/shard_map/pallas_call | solution.py:582
  51.4 3.0 %shard_map.112 = (bf16[48,4,2048]{2,1,0:T(4,128)(2,1)}, f32[2,1024,256]{2,1,0:T(8,128)}, f32[2,1024,256]{2,1,0:T(8,128)}, f32[2,1024,256]{2,1,0:T(8,128)}) custom-call(bf16[12,256,128]{2,1,0:T(8,128)(2,1)S(1)} %get-tuple-element.15.query_ref, f32[12,256,128]{2,1,0:T(8,128)S(1)} %get-tuple-element.16.old_ref, f32[12,256,128]{2,1,0:T(8,128)S(1)} %get-tuple-element.17.mass_ref, ...), custom_call_target="tpu_custom_call" | custom-call | tf_op jit(solution)/shard_map/pallas_call | solution.py:642

commit v4 on v3

--- a/solution.py
+++ b/solution.py
@@ -11,7 +11,7 @@
 MESH = pl.DeviceIdType.MESH
 W_CHUNKS = 4
 W_EARLY = 2
-GROUPS = 4
+GROUPS = 2
 ADAM_SUB = 32
 TAIL_ROWS = 8
 LOG2E = 1.4426950408889634
@@ -21,10 +21,10 @@
 def learner_kernel(
     lengths_hbm, grad_hbm, master_hbm, one_hbm, two_hbm, x_hbm, kv_hbm, q_hbm,
     fresh_out, query_out, old_out, mass_out, master_out, one_out, two_out,
-    own_grad, peer_grad, master, one, two, wpair, wbuf, xbuf, xflat,
-    far, far_peer, far_out, far_in, near, near_peer, kv_raw, q_raw, lengths, xstage,
-    grad_sem, state_sem, x_sem, kv_sem, out_sem, grad_send, grad_recv, x_send, x_recv, stage_send, stage_recv,
-    pair_send, pair_recv, w_send, w_recv, w_fwd_send, far_send, far_recv, back_send, back_recv, near_send, near_recv,
+    own_grad, peer_grad, master, one, two, wpair, wbuf, xbuf, xstage, xflat,
+    far, far_peer, far_out, far_in, near, near_peer, kv_raw, q_raw, lengths,
+    state_sem, local_sem, out_sem, grad_send, grad_recv, x_send, x_recv, stage_recv,
+    pair_send, pair_recv, w_send, w_near, w_diag, far_send, far_recv, back_send, back_recv, near_send, near_recv,
 ):
     r, f, t = lax.axis_index("rep"), lax.axis_index("fsdp"), lax.axis_index("tp")
     nf = 1 - f
@@ -54,7 +54,7 @@
 
     order = []
     for c in range(W_CHUNKS):
-        order += [(theirs, c), (mine, c)]
+        order += [(mine, c), (theirs, c)]
 
     def features(h, sub):
         return pl.ds(pl.multiple_of(h * depth + sub * half, half), half)
@@ -63,30 +63,31 @@
         return pl.ds(g * group_rows, group_rows)
 
     def tokens(g):
-        return pl.ds(pl.multiple_of(g * group_tokens, group_tokens), group_tokens)
-
-    grad_local, state_local = [], []
-    for i, (sub, c) in enumerate(order):
-        at = state_rows(sub, c)
-        source = pl.ds(pl.multiple_of(f * depth + sub * half + c * chunk, chunk), chunk)
-        grad_local.append(
-            pltpu.make_async_copy(grad_hbm.at[0, :, source, :], own_grad.at[:, at, :], grad_sem.at[i])
-        )
+        return pl.ds(g * group_tokens, group_tokens)
+
+    state_local = []
+    for i, sub in enumerate((mine, theirs)):
+        at = pl.ds(pl.multiple_of(sub * half, half), half)
+        source = pl.ds(pl.multiple_of(f * depth + sub * half, half), half)
         state_local.append([
-            pltpu.make_async_copy(hbm.at[:, at, :], vmem.at[:, at, :], state_sem.at[j, i])
-            for j, (hbm, vmem) in enumerate(((master_hbm, master), (one_hbm, one), (two_hbm, two)))
+            pltpu.make_async_copy(hbm, vmem, state_sem.at[j, i])
+            for j, (hbm, vmem) in enumerate((
+                (grad_hbm.at[0, :, source, :], own_grad.at[:, at, :]),
+                (master_hbm.at[:, at, :], master.at[:, at, :]),
+                (one_hbm.at[:, at, :], one.at[:, at, :]),
+                (two_hbm.at[:, at, :], two.at[:, at, :]),
+            ))
         ])
-        grad_local[i].start()
         for copy in state_local[i]:
             copy.start()
-    x_local = pltpu.make_async_copy(x_hbm.at[:, :, features(f, mine)], xbuf.at[t, f], x_sem.at[0])
-    kv_local = pltpu.make_async_copy(kv_hbm, kv_raw, kv_sem.at[0])
-    x_local.start()
-    kv_local.start()
-    q_local = pltpu.make_async_copy(q_hbm, q_raw, kv_sem.at[1])
-    q_local.start()
-    length_local = pltpu.make_async_copy(lengths_hbm, lengths, kv_sem.at[2])
-    length_local.start()
+    local = [
+        pltpu.make_async_copy(x_hbm.at[:, :, features(f, mine)], xbuf.at[t, f], local_sem.at[0]),
+        pltpu.make_async_copy(kv_hbm, kv_raw, local_sem.at[1]),
+        pltpu.make_async_copy(q_hbm, q_raw, local_sem.at[2]),
+        pltpu.make_async_copy(lengths_hbm, lengths, local_sem.at[3]),
+    ]
+    for copy in local:
+        copy.start()
 
     barrier = pltpu.get_barrier_semaphore()
     friends = [partner, dev_x, dev_y]
@@ -103,113 +104,81 @@
             device_id=device, device_id_type=MESH,
         )
 
+    def drain(ref, sem):
+        remote(ref, ref, sem, sem, partner).wait_send()
+
+    def landed(ref, sem):
+        remote(ref, ref, sem, sem, partner).wait_recv()
+
     def grad_copy(i):
         sub, c = order[i]
         source = pl.ds(pl.multiple_of(nf * depth + sub * half + c * chunk, chunk), chunk)
         return remote(
             grad_hbm.at[0, :, source, :], peer_grad.at[:, state_rows(sub, c), :],
-            grad_send.at[i], grad_recv.at[i], partner,
+            grad_send.at[0], grad_recv.at[i], partner,
         )
 
     def x_own(g, h, sub, slot, device):
-        return remote(
+        remote(
             x_hbm.at[some_rows(g), :, features(h, sub)], xbuf.at[t, f, some_rows(g)],
-            x_send.at[slot, g], x_recv.at[t, f, g], device,
-        )
+            x_send.at[slot], x_recv.at[t, g], device,
+        ).start()
 
     def x_swap(g):
-        return x_own(g, nf, mine, 0, partner)
-
-    def x_mirror(g, h):
-        return x_own(g, h, mine, 1 + h, (r, h, mirror))
+        x_own(g, nf, mine, 0, partner)
+
+    def x_mirror(g):
+        for h in range(2):
+            x_own(g, h, mine, 1, (r, h, mirror))
 
     def x_pair(g, h):
-        return x_own(g, h, theirs, 3 + h, (r, h, pair))
-
-    def x_pair_mirror(g, h):
-        return x_own(g, h, theirs, 5 + h, (r, h, pair_mirror))
-
-    def x_relay(g, th):
-        return remote(
-            xbuf.at[pair, th, some_rows(g)], xbuf.at[pair, th, some_rows(g)],
-            x_send.at[7 + th, g], x_recv.at[pair, th, g], (r, f, mirror),
-        )
-
-    def x_stage(g, h):
-        return remote(
-            x_hbm.at[some_rows(g), :, features(h, theirs)], xstage.at[f, some_rows(g)],
-            x_send.at[5 + h, g], stage_recv.at[f, g], (r, h, mirror),
-        )
-
-    def x_unstage(g, th):
-        return remote(
-            xstage.at[th, some_rows(g)], xbuf.at[mirror, th, some_rows(g)],
-            stage_send.at[th, g], x_recv.at[mirror, th, g], (r, f, pair),
-        )
-
-    def unstage(g):
-        for th in range(2):
-            remote(
-                xstage.at[th, some_rows(g)], xstage.at[th, some_rows(g)],
-                x_send.at[5, g], stage_recv.at[th, g], (r, f, mirror),
-            ).wait_recv()
-            x_unstage(g, th).start()
-
-    def x_arrived(k, th, g):
+        x_own(g, h, theirs, 2, (r, h, pair))
+
+    def x_pair_mirror(g):
+        for h in range(2):
+            x_own(g, h, theirs, 3, (r, h, pair_mirror))
+
+    def x_arrived(k, g):
+        landed(xbuf.at[k, :, some_rows(g)], x_recv.at[k, g])
+
+    def relay(g):
+        x_arrived(pair, g)
         remote(
-            xbuf.at[k, th, some_rows(g)], xbuf.at[k, th, some_rows(g)],
-            x_send.at[0, g], x_recv.at[k, th, g], partner,
-        ).wait_recv()
-
-    def go(make, groups):
-        for g in groups:
-            for h in range(2):
-                make(g, h).start()
-
-    every = range(GROUPS)
-    early = range(GROUPS // 2)
-    late = range(GROUPS // 2, GROUPS)
-
-    def relay(g):
-        for th in range(2):
-            x_arrived(pair, th, g)
-
-        for th in range(2):
-            x_relay(g, th).start()
+            xbuf.at[pair, :, some_rows(g)], xbuf.at[pair, :, some_rows(g)],
+            x_send.at[4], x_recv.at[pair, g], (r, f, mirror),
+        ).start()
+
+    def x_stage(h):
+        remote(
+            x_hbm.at[some_rows(0), :, features(h, theirs)], xstage.at[f],
+            x_send.at[3], stage_recv.at[0], (r, h, mirror),
+        ).start()
+
+    def unstage():
+        landed(xstage, stage_recv.at[0])
+        remote(
+            xstage, xbuf.at[mirror, :, some_rows(0)], x_send.at[5], x_recv.at[mirror, 0], (r, f, pair)
+        ).start()
 
     def w_pair(c):
         return remote(
             wpair.at[:, pl.ds(c * chunk, chunk), :], wbuf.at[1, :, owner_rows(r, c), :],
-            pair_send.at[c], pair_recv.at[c], (r, f, pair),
+            pair_send.at[0], pair_recv.at[c], (r, f, pair),
         )
 
-    def w_copy(cg, c, way):
-        return remote(
-            wbuf.at[cg, :, owner_rows(r, c), :], wbuf.at[cg, :, owner_rows(r, c), :],
-            w_send.at[cg, way, c], w_recv.at[cg, r, c], dev_x if way == 0 else dev_y,
-        )
-
-    def w_arrived(cg, owner, c):
-        remote(
-            wbuf.at[cg, :, owner_rows(owner, c), :], wbuf.at[cg, :, owner_rows(owner, c), :],
-            w_send.at[cg, 0, c], w_recv.at[cg, owner, c], dev_x,
-        ).wait_recv()
-
-    def w_forward(cg, c):
+    def w_go(cg, c):
+        at = wbuf.at[cg, :, owner_rows(r, c), :]
+        remote(at, at, w_send.at[0], w_near.at[cg, c], dev_x).start()
+        remote(at, at, w_send.at[1], w_near.at[cg, c], dev_y).start()
+
+    def w_step(cg, c):
+        landed(wbuf.at[cg, :, pl.ds(0, 2 * chunk), :], w_near.at[cg, c])
         owner, device = (rx, dev_y) if c % 2 == 0 else (ry, dev_x)
-        return remote(
-            wbuf.at[cg, :, owner_rows(owner, c), :], wbuf.at[cg, :, owner_rows(owner, c), :],
-            w_fwd_send.at[cg, c], w_recv.at[cg, owner, c], device,
-        )
-
-    def w_go(cg, c):
-        w_copy(cg, c, 0).start()
-        w_copy(cg, c, 1).start()
-
-    def w_step(cg, c):
-        w_arrived(cg, rx, c)
-        w_arrived(cg, ry, c)
-        w_forward(cg, c).start()
+        at = wbuf.at[cg, :, owner_rows(owner, c), :]
+        remote(at, at, w_send.at[2], w_diag.at[cg, c], device).start()
+
+    def w_last(cg, c):
+        landed(wbuf.at[cg, :, owner_rows(rd, c), :], w_diag.at[cg, c])
 
     def pair_step(c):
         w_pair(c).wait_recv()
@@ -219,18 +188,21 @@
 
     @pl.when(middle)
     def _():
-        go(x_pair, [0])
-        go(x_mirror, every)
-        go(x_stage, early)
+        x_pair(0, 0)
+        x_mirror(0)
+        x_mirror(1)
+        x_stage(0)
+        x_stage(1)
 
     @pl.when(jnp.logical_not(middle))
     def _():
-        go(x_pair, early)
+        x_pair(0, 0)
+        x_pair(0, 1)
 
     for i in range(1, len(order)):
         grad_copy(i).start()
     for g in range(GROUPS):
-        x_swap(g).start()
+        x_swap(g)
 
     first_bias = 1.0 - 0.9**10
     second_bias = 1.0 - 0.95**10
@@ -254,18 +226,17 @@
         lax.fori_loop(0, chunk // ADAM_SUB, piece, 0)
 
     for i, (sub, c) in enumerate(order):
-        grad_local[i].wait()
-        for copy in state_local[i]:
-            copy.wait()
+        if i < 2:
+            for copy in state_local[i]:
+                copy.wait()
         grad_copy(i).wait_recv()
-        if i % 2 == 0:
+        if i % 2 == 1:
             adam(sub, c, wpair, 0)
             w_pair(c).start()
         else:
             adam(sub, c, wbuf.at[0], r * half)
             if c < W_EARLY:
                 w_go(0, c)
-
     outs = [
         pltpu.make_async_copy(master, master_out, out_sem.at[0]),
         pltpu.make_async_copy(one, one_out, out_sem.at[1]),
@@ -273,10 +244,8 @@
     ]
     for copy in outs:
         copy.start()
-    x_local.wait()
-    kv_local.wait()
-    q_local.wait()
-    length_local.wait()
+    for copy in local:
+        copy.wait()
 
     kv_rows, cache_len = kv_raw.shape[:2]
     parts = kv_rows // TAIL_ROWS
@@ -324,12 +293,12 @@
 
     @pl.when(middle)
     def _():
-        for g in early:
-            relay(g)
+        relay(0)
 
     @pl.when(jnp.logical_not(middle))
     def _():
-        go(x_pair, late)
+        x_pair(1, 0)
+        x_pair(1, 1)
 
     def send_next(item):
         cg, c = item
@@ -340,98 +309,88 @@
 
     items = [(0, c) for c in range(W_EARLY)] + [(1, c) for c in range(W_CHUNKS)]
     items += [(0, c) for c in range(W_EARLY, W_CHUNKS)]
+    for c in range(W_EARLY):
+        w_step(0, c)
     for i in range(W_EARLY + W_CHUNKS):
-        w_step(*items[i])
-        if i + W_EARLY < len(items):
-            send_next(items[i + W_EARLY])
-            if items[i + W_EARLY] == (1, W_CHUNKS - 3):
-                @pl.when(middle)
-                def _():
-                    go(x_pair, every[1:])
-
-            if items[i + W_EARLY] == (1, W_CHUNKS - 2):
-                @pl.when(middle)
-                def _():
-                    for g in early:
-                        unstage(g)
-
-                @pl.when(jnp.logical_not(middle))
-                def _():
-                    go(x_mirror, early)
-
-            if items[i + W_EARLY] == (1, W_CHUNKS - 1):
-                @pl.when(middle)
-                def _():
-                    for g in late:
-                        relay(g)
-
-            if items[i + W_EARLY] == (0, W_EARLY):
-                @pl.when(middle)
-                def _():
-                    go(x_pair_mirror, late)
-
-                @pl.when(jnp.logical_not(middle))
-                def _():
-                    go(x_mirror, late)
+        if i >= W_EARLY:
+            w_step(*items[i])
+        upcoming = items[i + W_EARLY]
+        send_next(upcoming)
+        if upcoming == (1, W_CHUNKS - 3):
+            @pl.when(middle)
+            def _():
+                x_pair(0, 1)
+
+        if upcoming == (1, W_CHUNKS - 2):
+            @pl.when(middle)
+            def _():
+                unstage()
+                relay(1)
+
+            @pl.when(jnp.logical_not(middle))
+            def _():
+                x_mirror(0)
+
+        if upcoming == (1, W_CHUNKS - 1):
+            @pl.when(middle)
+            def _():
+                x_pair(1, 0)
+                x_pair(1, 1)
+
+        if upcoming == (0, W_EARLY):
+            @pl.when(middle)
+            def _():
+                x_pair_mirror(1)
+
+            @pl.when(jnp.logical_not(middle))
+            def _():
+                x_mirror(1)
 
         if i < parts:
             cached_part(i)
     for part in range(W_EARLY + W_CHUNKS, parts):
         cached_part(part)
-    for c in range(W_CHUNKS):
-        w_arrived(1, rd, c)
-    for c in range(W_EARLY):
-        w_arrived(0, rd, c)
-    for c in range(W_EARLY, W_CHUNKS - 1):
-        w_step(0, c)
 
     def far_swap(g):
         return remote(
-            far.at[nf, :, tokens(g), :], far_peer.at[:, tokens(g), :], far_send.at[g], far_recv.at[g], partner
+            far.at[nf, :, tokens(g), :], far_peer.at[:, tokens(g), :], far_send.at[0], far_recv.at[g], partner
         )
 
     def far_back(g):
         return remote(
-            far_out.at[:, tokens(g), :], far_in.at[:, tokens(g), :], back_send.at[g], back_recv.at[g], (r, f, pair)
+            far_out.at[:, tokens(g), :], far_in.at[:, tokens(g), :], back_send.at[0], back_recv.at[g], (r, f, pair)
         )
 
-    def near_part(lhs, kv, start, stop):
-        total = None
-        for k in range(blocks):
-            at = slice(k * half + start * chunk, k * half + stop * chunk)
-            product = jnp.dot(lhs[:, at], wbuf[0, kv, at, :], preferred_element_type=jnp.float32)
-            total = product if total is None else total + product
-        return total
-
-    def far_step(g, carry):
-        @pl.when(jnp.logical_not(middle))
-        def _():
+    def near_swap(g):
+        return remote(
+            near.at[nf, :, tokens(g), :], near_peer.at[:, tokens(g), :], near_send.at[0], near_recv.at[g], partner
+        )
+
+    def flatten(g):
+        def one_block(k, carry):
             for th in range(2):
-                x_arrived(pair, th, g)
-
-        x_arrived(t, nf, g)
-        for th in range(2):
-            x_arrived(mirror, th, g)
-            x_arrived(pair_mirror, th, g)
-
-        def flatten(k, inner):
+                piece = xbuf[k, th, some_rows(g)].reshape(group_tokens, half)
+                xflat[g, pl.ds(th * group_tokens, group_tokens), pl.ds(pl.multiple_of(k * half, half), half)] = piece
+            return carry
+
+        lax.fori_loop(0, blocks, one_block, 0)
+
+    def multiply(cg, out, g, start, stop):
+        for kv in range(2):
+            total = None
+            if stop - start == W_CHUNKS:
+                total = jnp.dot(xflat[g], wbuf[cg, kv], preferred_element_type=jnp.float32)
+            else:
+                for k in range(blocks):
+                    at = slice(k * half + start * chunk, k * half + stop * chunk)
+                    product = jnp.dot(xflat[g, :, at], wbuf[cg, kv, at, :], preferred_element_type=jnp.float32)
+                    total = product if total is None else total + product
             for th in range(2):
-                piece = xbuf[k, th, pl.ds(g * group_rows, group_rows)].reshape(group_tokens, half)
-                xflat[th, tokens(g), pl.ds(pl.multiple_of(k * half, half), half)] = piece
-            return inner
-
-        lax.fori_loop(0, blocks, flatten, 0)
-        lhs = jnp.concatenate([xflat[0, tokens(g), :], xflat[1, tokens(g), :]], axis=0)
-        for kv in range(2):
-            product = jnp.dot(lhs, wbuf[1, kv], preferred_element_type=jnp.float32)
-            for th in range(2):
-                far[th, kv, tokens(g), :] = product[th * group_tokens : (th + 1) * group_tokens]
-        far_swap(g).start()
-        for kv in range(2):
-            product = near_part(lhs, kv, 0, W_EARLY)
-            for th in range(2):
-                near[th, kv, tokens(g), :] = product[th * group_tokens : (th + 1) * group_tokens]
-        return carry
+                piece = total[th * group_tokens : (th + 1) * group_tokens]
+                if start > 0:
+                    out[th, kv, tokens(g), :] += piece
+                else:
+                    out[th, kv, tokens(g), :] = piece
 
     def far_done(g):
         far_swap(g).wait_recv()
@@ -439,73 +398,92 @@
         far_out[:, tokens(g), :] = both.astype(jnp.bfloat16)
         far_back(g).start()
 
-    def far_loop(g, carry):
-        far_step(g, 0)
-
-        @pl.when(g > 0)
-        def _():
-            far_done(g - 1)
-
-        @pl.when(g == 0)
-        def _():
-            w_step(0, W_CHUNKS - 1)
-
-        return carry
-
-    lax.fori_loop(0, GROUPS, far_loop, 0)
-    far_done(GROUPS - 1)
-
-    near_swap = remote(near.at[nf], near_peer, near_send.at[0], near_recv.at[0], partner)
+    def x_ready(g):
+        landed(xbuf.at[t, nf, some_rows(g)], x_recv.at[t, g])
+        x_arrived(mirror, g)
+        x_arrived(pair_mirror, g)
+        flatten(g)
+
+    for c in range(W_EARLY):
+        w_last(0, c)
+        w_last(1, c)
+
+    @pl.when(jnp.logical_not(middle))
+    def _():
+        x_arrived(pair, 0)
+
+    x_ready(0)
+    multiply(1, far, 0, 0, W_EARLY)
+    multiply(0, near, 0, 0, W_EARLY)
+
+    for c in range(W_EARLY, W_CHUNKS - 1):
+        w_step(0, c)
+
+    @pl.when(middle)
+    def _():
+        x_ready(1)
+        multiply(1, far, 1, 0, W_EARLY)
+
     for c in range(W_EARLY, W_CHUNKS):
-        w_arrived(0, rd, c)
-
-    def near_last(i, carry):
-        th = jnp.where(i == 0, nf, f)
-        for kv in range(2):
-            near[th, kv] += near_part(xflat.at[th], kv, W_EARLY, W_CHUNKS)
-
-        @pl.when(i == 0)
-        def _():
-            near_swap.start()
-
-        return carry
-
-    lax.fori_loop(0, 2, near_last, 0)
-
-    for i in range(len(order)):
-        grad_copy(i).wait_send()
-    for c in range(W_CHUNKS):
-        w_pair(c).wait_send()
-        for cg in range(2):
-            w_copy(cg, c, 0).wait_send()
-            w_copy(cg, c, 1).wait_send()
-            w_forward(cg, c).wait_send()
+        w_last(1, c)
+    multiply(1, far, 0, W_EARLY, W_CHUNKS)
+    far_swap(0).start()
+
+    @pl.when(middle)
+    def _():
+        multiply(1, far, 1, W_EARLY, W_CHUNKS)
+        far_swap(1).start()
+
+    far_done(0)
+    w_step(0, W_CHUNKS - 1)
+
+    @pl.when(jnp.logical_not(middle))
+    def _():
+        x_arrived(pair, 1)
+        x_ready(1)
+        multiply(1, far, 1, 0, W_CHUNKS)
+        far_swap(1).start()
+
+    @pl.when(middle)
+    def _():
+        far_done(1)
+
+    multiply(0, near, 1, 0, W_EARLY)
+
+    @pl.when(jnp.logical_not(middle))
+    def _():
+        far_done(1)
+
+    for c in range(W_EARLY, W_CHUNKS):
+        w_last(0, c)
     for g in range(GROUPS):
-        x_swap(g).wait_send()
-        for h in range(2):
-            x_pair(g, h).wait_send()
-            x_mirror(g, h).wait_send()
-        far_swap(g).wait_send()
-        far_back(g).wait_send()
+        multiply(0, near, g, W_EARLY, W_CHUNKS)
+        near_swap(g).start()
+
+    drain(peer_grad, grad_send.at[0])
+    drain(xbuf.at[0, 0], x_send.at[0])
+    drain(xbuf.at[0], x_send.at[1])
+    drain(xbuf.at[0], x_send.at[2])
 
     @pl.when(middle)
     def _():
-        for h in range(2):
-            for g in every:
-                x_relay(g, h).wait_send()
-            for g in early:
-                x_stage(g, h).wait_send()
-                x_unstage(g, h).wait_send()
-            for g in late:
-                x_pair_mirror(g, h).wait_send()
-
+        drain(xbuf.at[0], x_send.at[3])
+        drain(xbuf.at[0], x_send.at[4])
+        drain(xstage, x_send.at[5])
+
+    drain(wpair, pair_send.at[0])
+    for way in range(3):
+        drain(wbuf.at[:, :, pl.ds(0, half), :], w_send.at[way])
+    drain(far.at[0], far_send.at[0])
+    drain(far_out, back_send.at[0])
     for copy in outs:
         copy.wait()
     for g in range(GROUPS):
+        near_swap(g).wait_recv()
+    for g in range(GROUPS):
         far_back(g).wait_recv()
-    near_swap.wait_recv()
     fresh_out[...] = (near[f] + near_peer[...] + far_in[...].astype(jnp.float32)).astype(jnp.bfloat16)
-    near_swap.wait_send()
+    drain(near.at[0], near_send.at[0])
 
 
 def tail_kernel(
@@ -601,7 +579,8 @@
             pltpu.VMEM((2, half, width), bf16),
             pltpu.VMEM((2, 2, n_rep * half, width), bf16),
             pltpu.VMEM((n_tp, 2, row_count, step_count, half), bf16),
-            pltpu.VMEM((2, tokens, n_tp * half), bf16),
+            pltpu.VMEM((2, row_count // GROUPS, step_count, half), bf16),
+            pltpu.VMEM((GROUPS, 2 * tokens // GROUPS, n_tp * half), bf16),
             pltpu.VMEM((2, 2, tokens, width), f32),
             pltpu.VMEM((2, tokens, width), f32),
             pltpu.VMEM((2, tokens, width), bf16),
@@ -611,29 +590,25 @@
             pltpu.VMEM(kv_cache.shape, bf16),
             pltpu.VMEM(queries.shape, bf16),
             pltpu.SMEM(lengths.shape, jnp.int32),
-            pltpu.VMEM((2, row_count, step_count, half), bf16),
+            dma((4, 2)),
+            dma((4,)),
+            dma((3,)),
+            dma((1,)),
             dma((2 * W_CHUNKS,)),
-            dma((3, 2 * W_CHUNKS)),
+            dma((6,)),
+            dma((n_tp, GROUPS)),
             dma((1,)),
+            dma((1,)),
+            dma((W_CHUNKS,)),
             dma((3,)),
-            dma((3,)),
-            dma((2 * W_CHUNKS,)),
-            dma((2 * W_CHUNKS,)),
-            dma((9, GROUPS)),
-            dma((n_tp, 2, GROUPS)),
-            dma((2, GROUPS)),
-            dma((2, GROUPS)),
-            dma((W_CHUNKS,)),
-            dma((W_CHUNKS,)),
-            dma((2, 2, W_CHUNKS)),
-            dma((2, n_rep, W_CHUNKS)),
             dma((2, W_CHUNKS)),
-            dma((GROUPS,)),
-            dma((GROUPS,)),
-            dma((GROUPS,)),
+            dma((2, W_CHUNKS)),
+            dma((1,)),
             dma((GROUPS,)),
             dma((1,)),
+            dma((GROUPS,)),
             dma((1,)),
+            dma((GROUPS,)),
         ],
         compiler_params=pltpu.CompilerParams(
             collective_id=0, has_side_effects=True, vmem_limit_bytes=36 * 1024 * 1024

time: 54.7 us -> 53.5 us (0.978)
  Pallas kernels: 53.7 us -> 52.7 us
    pallas_call x1, Pallas kernels: 50.8 us -> 49.7 us  [fused_device(): pl.pallas_call(learner_kernel, out_shape=(jax.ShapeDtypeStruct((2, tokens...]
where the time goes in v4:
time: 53.5 us; the launch traced here: 53.3 us
  Pallas kernels  52.7 us (99%)
  between operations  0.64 us (1%)
    pallas_call x1, Pallas kernels, fused_device(): pl.pallas_call(learner_kernel, out_shape=(jax.ShapeDtypeStruct((2, tokens...  49.7 us
    pallas_call x1, Pallas kernels, fused_device(): pl.pallas_call(tail_kernel, out_shape=(jax.ShapeDtypeStruct(queries.shape...  2.98 us

profile of v4, /device:TPU:0, one launch (start us, length us, event | category | flops | bytes accessed | tf_op | source)
XLA Modules:
  0.0 53.3 jit_solution(11197739163627515772)
XLA Ops:
  0.6 49.7 %shard_map.111 = (bf16[2,192,256]{2,1,0:T(8,128)(2,1)S(1)}, bf16[12,256,128]{2,1,0:T(8,128)(2,1)S(1)}, f32[12,256,128]{2,1,0:T(8,128)S(1)}, f32[12,256,128]{2,1,...) custom-call(s32[48]{0:T(128)} %lengths_hbm.1, ...), custom_call_target="tpu_custom_call" | custom-call | tf_op jit(solution)/shard_map/pallas_call | solution.py:560
  50.3 3.0 %shard_map.112 = (bf16[48,4,2048]{2,1,0:T(4,128)(2,1)}, f32[2,1024,256]{2,1,0:T(8,128)}, f32[2,1024,256]{2,1,0:T(8,128)}, f32[2,1024,256]{2,1,0:T(8,128)}) custom-call(bf16[12,256,128]{2,1,0:T(8,128)(2,1)S(1)} %get-tuple-element.15.query_ref, f32[12,256,128]{2,1,0:T(8,128)S(1)} %get-tuple-element.16.old_ref, f32[12,256,128]{2,1,0:T(8,128)S(1)} %get-tuple-element.17.mass_ref, ...), custom_call_target="tpu_custom_call" | custom-call | tf_op jit(solution)/shard_map/pallas_call | solution.py:617

commit v5 on v4

--- a/solution.py
+++ b/solution.py
@@ -11,6 +11,7 @@
 MESH = pl.DeviceIdType.MESH
 W_CHUNKS = 4
 W_EARLY = 2
+W_AHEAD = 2
 GROUPS = 2
 ADAM_SUB = 32
 TAIL_ROWS = 8
@@ -24,7 +25,7 @@
     own_grad, peer_grad, master, one, two, wpair, wbuf, xbuf, xstage, xflat,
     far, far_peer, far_out, far_in, near, near_peer, kv_raw, q_raw, lengths,
     state_sem, local_sem, out_sem, grad_send, grad_recv, x_send, x_recv, stage_recv,
-    pair_send, pair_recv, w_send, w_near, w_diag, far_send, far_recv, back_send, back_recv, near_send, near_recv,
+    pair_send, pair_recv, w_send, w_near, w_diag, far_send, far_recv, back_send, back_recv, near_send, near_recv, hello,
 ):
     r, f, t = lax.axis_index("rep"), lax.axis_index("fsdp"), lax.axis_index("tp")
     nf = 1 - f
@@ -86,17 +87,24 @@
         pltpu.make_async_copy(q_hbm, q_raw, local_sem.at[2]),
         pltpu.make_async_copy(lengths_hbm, lengths, local_sem.at[3]),
     ]
-    for copy in local:
-        copy.start()
-
     barrier = pltpu.get_barrier_semaphore()
-    friends = [partner, dev_x, dev_y]
-    for i in range(1, blocks):
+
+    def greet(device):
+        pl.semaphore_signal(barrier, inc=1, device_id=device, device_id_type=MESH)
+
+    for device in (partner, dev_x, dev_y, (r, 0, pair), (r, 1, pair)):
+        greet(device)
+
+    @pl.when(middle)
+    def _():
         for h in range(2):
-            friends.append((r, h, lax.rem(t + i, blocks)))
-    for device in friends:
-        pl.semaphore_signal(barrier, inc=1, device_id=device, device_id_type=MESH)
-    pl.semaphore_wait(barrier, len(friends))
+            greet((r, h, mirror))
+
+    pl.semaphore_wait(barrier, jnp.where(middle, 7, 5))
+
+    @pl.when(middle)
+    def _():
+        pl.semaphore_signal(hello.at[0], inc=1, device_id=(r, f, mirror), device_id_type=MESH)
 
     def remote(src, dst, send, recv, device):
         return pltpu.make_async_remote_copy(
@@ -173,9 +181,9 @@
 
     def w_step(cg, c):
         landed(wbuf.at[cg, :, pl.ds(0, 2 * chunk), :], w_near.at[cg, c])
-        owner, device = (rx, dev_y) if c % 2 == 0 else (ry, dev_x)
-        at = wbuf.at[cg, :, owner_rows(owner, c), :]
-        remote(at, at, w_send.at[2], w_diag.at[cg, c], device).start()
+        for kv, owner, device in ((0, rx, dev_y), (1, ry, dev_x)):
+            at = wbuf.at[cg, kv, owner_rows(owner, c), :]
+            remote(at, at, w_send.at[2], w_diag.at[cg, c], device).start()
 
     def w_last(cg, c):
         landed(wbuf.at[cg, :, owner_rows(rd, c), :], w_diag.at[cg, c])
@@ -201,8 +209,6 @@
 
     for i in range(1, len(order)):
         grad_copy(i).start()
-    for g in range(GROUPS):
-        x_swap(g)
 
     first_bias = 1.0 - 0.9**10
     second_bias = 1.0 - 0.95**10
@@ -242,10 +248,10 @@
         pltpu.make_async_copy(one, one_out, out_sem.at[1]),
         pltpu.make_async_copy(two, two_out, out_sem.at[2]),
     ]
-    for copy in outs:
+    for copy in local:
         copy.start()
-    for copy in local:
-        copy.wait()
+    for g in range(GROUPS):
+        x_swap(g)
 
     kv_rows, cache_len = kv_raw.shape[:2]
     parts = kv_rows // TAIL_ROWS
@@ -293,6 +299,8 @@
 
     @pl.when(middle)
     def _():
+        pl.semaphore_wait(hello.at[0], 1)
+        pl.semaphore_signal(hello.at[1], inc=1, device_id=(r, f, pair), device_id_type=MESH)
         relay(0)
 
     @pl.when(jnp.logical_not(middle))
@@ -309,42 +317,43 @@
 
     items = [(0, c) for c in range(W_EARLY)] + [(1, c) for c in range(W_CHUNKS)]
     items += [(0, c) for c in range(W_EARLY, W_CHUNKS)]
+    sent = W_EARLY
     for c in range(W_EARLY):
         w_step(0, c)
+    for copy in local:
+        copy.wait()
     for i in range(W_EARLY + W_CHUNKS):
         if i >= W_EARLY:
             w_step(*items[i])
-        upcoming = items[i + W_EARLY]
-        send_next(upcoming)
-        if upcoming == (1, W_CHUNKS - 3):
+        while sent < min(i + W_AHEAD + 1, len(items)):
+            send_next(items[sent])
+            sent += 1
+        if i == 1:
             @pl.when(middle)
             def _():
                 x_pair(0, 1)
-
-        if upcoming == (1, W_CHUNKS - 2):
-            @pl.when(middle)
-            def _():
                 unstage()
-                relay(1)
-
-            @pl.when(jnp.logical_not(middle))
-            def _():
-                x_mirror(0)
-
-        if upcoming == (1, W_CHUNKS - 1):
+
+        if i == 2:
             @pl.when(middle)
             def _():
                 x_pair(1, 0)
                 x_pair(1, 1)
-
-        if upcoming == (0, W_EARLY):
+                relay(1)
+
+            @pl.when(jnp.logical_not(middle))
+            def _():
+                pl.semaphore_wait(hello.at[1], 1)
+                x_mirror(0)
+                x_mirror(1)
+
+        if i == 3:
+            for copy in outs:
+                copy.start()
+
             @pl.when(middle)
             def _():
                 x_pair_mirror(1)
-
-            @pl.when(jnp.logical_not(middle))
-            def _():
-                x_mirror(1)
 
         if i < parts:
             cached_part(i)
@@ -408,16 +417,21 @@
         w_last(0, c)
         w_last(1, c)
 
-    @pl.when(jnp.logical_not(middle))
-    def _():
-        x_arrived(pair, 0)
-
-    x_ready(0)
-    multiply(1, far, 0, 0, W_EARLY)
-    multiply(0, near, 0, 0, W_EARLY)
+    @pl.when(middle)
+    def _():
+        x_ready(0)
+        multiply(1, far, 0, 0, W_EARLY)
+        multiply(0, near, 0, 0, W_EARLY)
 
     for c in range(W_EARLY, W_CHUNKS - 1):
         w_step(0, c)
+
+    @pl.when(jnp.logical_not(middle))
+    def _():
+        x_arrived(pair, 0)
+        x_ready(0)
+        multiply(1, far, 0, 0, W_EARLY)
+        multiply(0, near, 0, 0, W_EARLY)
 
     @pl.when(middle)
     def _():
@@ -609,6 +623,7 @@
             dma((GROUPS,)),
             dma((1,)),
             dma((GROUPS,)),
+            pltpu.SemaphoreType.REGULAR((2,)),
         ],
         compiler_params=pltpu.CompilerParams(
             collective_id=0, has_side_effects=True, vmem_limit_bytes=36 * 1024 * 1024

time: 53.5 us -> 52.5 us (0.981)
  Pallas kernels: 52.7 us -> 51.7 us
    pallas_call x1, Pallas kernels: 49.7 us -> 48.7 us  [fused_device(): pl.pallas_call(learner_kernel, out_shape=(jax.ShapeDtypeStruct((2, tokens...]
where the time goes in v5:
time: 52.5 us; the launch traced here: 52.4 us
  Pallas kernels  51.7 us (98%)
  between operations  0.64 us (1%)
    pallas_call x1, Pallas kernels, fused_device(): pl.pallas_call(learner_kernel, out_shape=(jax.ShapeDtypeStruct((2, tokens...  48.7 us
    pallas_call x1, Pallas kernels, fused_device(): pl.pallas_call(tail_kernel, out_shape=(jax.ShapeDtypeStruct(queries.shape...  2.98 us

profile of v5, /device:TPU:0, one launch (start us, length us, event | category | flops | bytes accessed | tf_op | source)
XLA Modules:
  0.0 52.4 jit_solution(9664895308648517455)
XLA Ops:
  0.6 48.7 %shard_map.111 = (bf16[2,192,256]{2,1,0:T(8,128)(2,1)S(1)}, bf16[12,256,128]{2,1,0:T(8,128)(2,1)S(1)}, f32[12,256,128]{2,1,0:T(8,128)S(1)}, f32[12,256,128]{2,1,...) custom-call(s32[48]{0:T(128)} %lengths_hbm.1, ...), custom_call_target="tpu_custom_call" | custom-call | tf_op jit(solution)/shard_map/pallas_call | solution.py:574
  49.4 3.0 %shard_map.112 = (bf16[48,4,2048]{2,1,0:T(4,128)(2,1)}, f32[2,1024,256]{2,1,0:T(8,128)}, f32[2,1024,256]{2,1,0:T(8,128)}, f32[2,1024,256]{2,1,0:T(8,128)}) custom-call(bf16[12,256,128]{2,1,0:T(8,128)(2,1)S(1)} %get-tuple-element.15.query_ref, f32[12,256,128]{2,1,0:T(8,128)S(1)} %get-tuple-element.16.old_ref, f32[12,256,128]{2,1,0:T(8,128)S(1)} %get-tuple-element.17.mass_ref, ...), custom_call_target="tpu_custom_call" | custom-call | tf_op jit(solution)/shard_map/pallas_call | solution.py:632

commit v6 on v5

--- a/solution.py
+++ b/solution.py
@@ -66,6 +66,19 @@
     def tokens(g):
         return pl.ds(g * group_tokens, group_tokens)
 
+    barrier = pltpu.get_barrier_semaphore()
+
+    def greet(device):
+        pl.semaphore_signal(barrier, inc=1, device_id=device, device_id_type=MESH)
+
+    for device in (partner, dev_x, dev_y, (r, 0, pair), (r, 1, pair)):
+        greet(device)
+
+    @pl.when(middle)
+    def _():
+        for h in range(2):
+            greet((r, h, mirror))
+
     state_local = []
     for i, sub in enumerate((mine, theirs)):
         at = pl.ds(pl.multiple_of(sub * half, half), half)
@@ -87,19 +100,6 @@
         pltpu.make_async_copy(q_hbm, q_raw, local_sem.at[2]),
         pltpu.make_async_copy(lengths_hbm, lengths, local_sem.at[3]),
     ]
-    barrier = pltpu.get_barrier_semaphore()
-
-    def greet(device):
-        pl.semaphore_signal(barrier, inc=1, device_id=device, device_id_type=MESH)
-
-    for device in (partner, dev_x, dev_y, (r, 0, pair), (r, 1, pair)):
-        greet(device)
-
-    @pl.when(middle)
-    def _():
-        for h in range(2):
-            greet((r, h, mirror))
-
     pl.semaphore_wait(barrier, jnp.where(middle, 7, 5))
 
     @pl.when(middle)
@@ -140,11 +140,11 @@
             x_own(g, h, mine, 1, (r, h, mirror))
 
     def x_pair(g, h):
-        x_own(g, h, theirs, 2, (r, h, pair))
+        x_own(g, h, theirs, 1, (r, h, pair))
 
     def x_pair_mirror(g):
         for h in range(2):
-            x_own(g, h, theirs, 3, (r, h, pair_mirror))
+            x_own(g, h, theirs, 2, (r, h, pair_mirror))
 
     def x_arrived(k, g):
         landed(xbuf.at[k, :, some_rows(g)], x_recv.at[k, g])
@@ -153,19 +153,19 @@
         x_arrived(pair, g)
         remote(
             xbuf.at[pair, :, some_rows(g)], xbuf.at[pair, :, some_rows(g)],
-            x_send.at[4], x_recv.at[pair, g], (r, f, mirror),
+            x_send.at[2], x_recv.at[pair, g], (r, f, mirror),
         ).start()
 
     def x_stage(h):
         remote(
             x_hbm.at[some_rows(0), :, features(h, theirs)], xstage.at[f],
-            x_send.at[3], stage_recv.at[0], (r, h, mirror),
+            x_send.at[2], stage_recv.at[0], (r, h, mirror),
         ).start()
 
     def unstage():
         landed(xstage, stage_recv.at[0])
         remote(
-            xstage, xbuf.at[mirror, :, some_rows(0)], x_send.at[5], x_recv.at[mirror, 0], (r, f, pair)
+            xstage, xbuf.at[mirror, :, some_rows(0)], x_send.at[3], x_recv.at[mirror, 0], (r, f, pair)
         ).start()
 
     def w_pair(c):
@@ -177,16 +177,16 @@
     def w_go(cg, c):
         at = wbuf.at[cg, :, owner_rows(r, c), :]
         remote(at, at, w_send.at[0], w_near.at[cg, c], dev_x).start()
-        remote(at, at, w_send.at[1], w_near.at[cg, c], dev_y).start()
+        remote(at, at, w_send.at[0], w_near.at[cg, c], dev_y).start()
 
     def w_step(cg, c):
         landed(wbuf.at[cg, :, pl.ds(0, 2 * chunk), :], w_near.at[cg, c])
         for kv, owner, device in ((0, rx, dev_y), (1, ry, dev_x)):
             at = wbuf.at[cg, kv, owner_rows(owner, c), :]
-            remote(at, at, w_send.at[2], w_diag.at[cg, c], device).start()
-
-    def w_last(cg, c):
-        landed(wbuf.at[cg, :, owner_rows(rd, c), :], w_diag.at[cg, c])
+            remote(at, at, w_send.at[0], w_diag.at[cg, c // W_EARLY], device).start()
+
+    def w_last(cg, late):
+        landed(wbuf.at[cg, :, pl.ds(0, W_EARLY * chunk), :], w_diag.at[cg, late])
 
     def pair_step(c):
         w_pair(c).wait_recv()
@@ -197,10 +197,10 @@
     @pl.when(middle)
     def _():
         x_pair(0, 0)
+        x_stage(0)
+        x_stage(1)
         x_mirror(0)
         x_mirror(1)
-        x_stage(0)
-        x_stage(1)
 
     @pl.when(jnp.logical_not(middle))
     def _():
@@ -345,15 +345,19 @@
             def _():
                 pl.semaphore_wait(hello.at[1], 1)
                 x_mirror(0)
-                x_mirror(1)
 
         if i == 3:
             for copy in outs:
                 copy.start()
 
+        if i == 4:
             @pl.when(middle)
             def _():
                 x_pair_mirror(1)
+
+            @pl.when(jnp.logical_not(middle))
+            def _():
+                x_mirror(1)
 
         if i < parts:
             cached_part(i)
@@ -413,9 +417,8 @@
         x_arrived(pair_mirror, g)
         flatten(g)
 
-    for c in range(W_EARLY):
-        w_last(0, c)
-        w_last(1, c)
+    w_last(0, 0)
+    w_last(1, 0)
 
     @pl.when(middle)
     def _():
@@ -433,19 +436,14 @@
         multiply(1, far, 0, 0, W_EARLY)
         multiply(0, near, 0, 0, W_EARLY)
 
-    @pl.when(middle)
-    def _():
-        x_ready(1)
-        multiply(1, far, 1, 0, W_EARLY)
-
-    for c in range(W_EARLY, W_CHUNKS):
-        w_last(1, c)
+    w_last(1, 1)
     multiply(1, far, 0, W_EARLY, W_CHUNKS)
     far_swap(0).start()
 
     @pl.when(middle)
     def _():
-        multiply(1, far, 1, W_EARLY, W_CHUNKS)
+        x_ready(1)
+        multiply(1, far, 1, 0, W_CHUNKS)
         far_swap(1).start()
 
     far_done(0)
@@ -468,28 +466,23 @@
     def _():
         far_done(1)
 
-    for c in range(W_EARLY, W_CHUNKS):
-        w_last(0, c)
+    w_last(0, 1)
     for g in range(GROUPS):
         multiply(0, near, g, W_EARLY, W_CHUNKS)
         near_swap(g).start()
 
     drain(peer_grad, grad_send.at[0])
     drain(xbuf.at[0, 0], x_send.at[0])
-    drain(xbuf.at[0], x_send.at[1])
-    drain(xbuf.at[0], x_send.at[2])
+    drain(xbuf.at[pl.ds(0, 2)], x_send.at[1])
 
     @pl.when(middle)
     def _():
-        drain(xbuf.at[0], x_send.at[3])
-        drain(xbuf.at[0], x_send.at[4])
-        drain(xstage, x_send.at[5])
+        drain(xbuf.at[pl.ds(0, 2)], x_send.at[2])
+        drain(xstage, x_send.at[3])
 
     drain(wpair, pair_send.at[0])
-    for way in range(3):
-        drain(wbuf.at[:, :, pl.ds(0, half), :], w_send.at[way])
+    drain(wbuf.at[:, :, pl.ds(0, 3 * half), :], w_send.at[0])
     drain(far.at[0], far_send.at[0])
-    drain(far_out, back_send.at[0])
     for copy in outs:
         copy.wait()
     for g in range(GROUPS):
@@ -498,6 +491,7 @@
         far_back(g).wait_recv()
     fresh_out[...] = (near[f] + near_peer[...] + far_in[...].astype(jnp.float32)).astype(jnp.bfloat16)
     drain(near.at[0], near_send.at[0])
+    drain(far_out, back_send.at[0])
 
 
 def tail_kernel(
@@ -609,14 +603,14 @@
             dma((3,)),
             dma((1,)),
             dma((2 * W_CHUNKS,)),
-            dma((6,)),
+            dma((4,)),
             dma((n_tp, GROUPS)),
             dma((1,)),
             dma((1,)),
             dma((W_CHUNKS,)),
-            dma((3,)),
+            dma((1,)),
             dma((2, W_CHUNKS)),
-            dma((2, W_CHUNKS)),
+            dma((2, 2)),
             dma((1,)),
             dma((GROUPS,)),
             dma((1,)),

time: 52.5 us -> 52.4 us (level)
  no operation moved by 1% of the time
where the time goes in v6:
time: 52.4 us; the launch traced here: 52.3 us
  Pallas kernels  51.6 us (98%)
  between operations  0.64 us (1%)
    pallas_call x1, Pallas kernels, fused_device(): pl.pallas_call(learner_kernel, out_shape=(jax.ShapeDtypeStruct((2, tokens...  48.6 us
    pallas_call x1, Pallas kernels, fused_device(): pl.pallas_call(tail_kernel, out_shape=(jax.ShapeDtypeStruct(queries.shape...  2.98 us

profile of v6, /device:TPU:0, one launch (start us, length us, event | category | flops | bytes accessed | tf_op | source)
XLA Modules:
  0.0 52.3 jit_solution(11963775401174887431)
XLA Ops:
  0.6 48.6 %shard_map.111 = (bf16[2,192,256]{2,1,0:T(8,128)(2,1)S(1)}, bf16[12,256,128]{2,1,0:T(8,128)(2,1)S(1)}, f32[12,256,128]{2,1,0:T(8,128)S(1)}, f32[12,256,128]{2,1,...) custom-call(s32[48]{0:T(128)} %lengths_hbm.1, ...), custom_call_target="tpu_custom_call" | custom-call | tf_op jit(solution)/shard_map/pallas_call | solution.py:568
  49.3 3.0 %shard_map.112 = (bf16[48,4,2048]{2,1,0:T(4,128)(2,1)}, f32[2,1024,256]{2,1,0:T(8,128)}, f32[2,1024,256]{2,1,0:T(8,128)}, f32[2,1024,256]{2,1,0:T(8,128)}) custom-call(bf16[12,256,128]{2,1,0:T(8,128)(2,1)S(1)} %get-tuple-element.15.query_ref, f32[12,256,128]{2,1,0:T(8,128)S(1)} %get-tuple-element.16.old_ref, f32[12,256,128]{2,1,0:T(8,128)S(1)} %get-tuple-element.17.mass_ref, ...), custom_call_target="tpu_custom_call" | custom-call | tf_op jit(solution)/shard_map/pallas_call | solution.py:626
